TPU v7x, 1024 devices: a whole 8x8x8 slice. The times are simulated.
1024 devices in a mesh: row: 8 (over y_hi, core), src: 128 (over z, y_lo, x).
Axes of the slice: x: 8, y: 8 (y_hi: 4, y_lo: 2; y = y_hi * 2 + y_lo), z: 8, core: 2. Of those that a mesh axis runs over, the one named last changes fastest.
Arguments:
- front_panel: float32 [3, 256, 16384], P(None, None, ('row', 'src')), may hold values from -0.046875 to 0.046875
- solved_prev: float32 [16384, 32768], P('row', 'src'), may hold values from -6 to 6
- right_side: float32 [768, 32768], P(None, 'src'), may hold values from -6 to 6
- front_window: float32 [768, 768], replicated, may hold values from -0.21875 to 0.21875
- inv_diag: float32 [3, 256, 256], replicated, may hold values from -0.375 to 0.375
- owner_map: int32 [3], replicated, may hold values from 0 to 7, as said below
Outputs:
- stored: float32 [2048, 32768], P('row', 'src')
Inputs may be any that keep to these rules, and one draw needn't show every extreme that they name: `owner_map`: the blocks' owners are distinct row groups.
All inputs are finite; a program needn't handle non-finite values.
Results may differ from a plain program's by a relative error of at most 0.0001.
Values sent between devices are 32-bit elements; how exact they have to be, the bound alone decides.
No kernel may reach another device: no remote copies, remote signals or barrier semaphores. Data moves between devices by JAX's collectives and lax.ppermute only.
A program may use at most 64 MiB of HBM per device.

v0:
```python
import jax
import jax.numpy as jnp
from jax import lax
from jax.sharding import Mesh
from jax.sharding import PartitionSpec as P

SRC = ("src_0", "src_1", "src_2")
ROW_SRC = ("row", "src_0", "src_1", "src_2")


def joined_along(pieces, dim):
    shape = list(pieces.shape[1:])
    shape[dim] *= pieces.shape[0]
    return jnp.moveaxis(pieces, 0, dim).reshape(shape)


def all_blocks(shard, axes, sequence):
    pieces = shard[None]
    for k in sequence:
        pieces = lax.all_gather(pieces, axes[k], axis=0, tiled=True)
    block = [lax.axis_size(axes[k]) for k in reversed(sequence)]
    pieces = pieces.reshape(*block, *shard.shape)
    turned = sorted(range(len(sequence)), key=lambda place: sequence[len(sequence) - 1 - place])
    return pieces.transpose(*turned, *range(len(sequence), pieces.ndim)).reshape(-1, *shard.shape)


def gather_axes(shard, axes, sequence, dim):
    return joined_along(all_blocks(shard, axes, sequence), dim)


def copy_for_each(shard, axis):
    peers = lax.axis_size(axis)
    return lax.all_to_all(
        jnp.broadcast_to(shard[None], (peers, *shard.shape)), axis, 0, 0, tiled=True
    )


def taken_together(shard, axis):
    return copy_for_each(shard, axis).sum(axis=0)


def body(front_panel, solved_prev, right_side, front_window, inv_diag, owner_map):
    highest = lax.Precision.HIGHEST
    nblk = front_panel.shape[0]
    block = front_panel.shape[1]
    width = solved_prev.shape[1]
    here = lax.axis_index("row")
    panel_rows = gather_axes(front_panel, SRC, (1, 0, 2), 2)
    local = jnp.einsum(
        "kbn,ns->kbs",
        panel_rows,
        solved_prev,
        precision=highest,
        preferred_element_type=jnp.float32,
    )
    partials = taken_together(local, "row")
    stored = jnp.zeros((block, width), jnp.float32)
    solutions = []
    for k in range(nblk):
        partial_value = partials[k]
        rhs = right_side[k * block : (k + 1) * block] - partial_value
        if k > 0:
            earlier = jnp.concatenate(solutions, axis=0)
            rhs = rhs - jnp.dot(
                front_window[k * block : (k + 1) * block, : k * block],
                earlier,
                precision=highest,
                preferred_element_type=jnp.float32,
            )
        mine = here == owner_map[k]
        solution = jnp.dot(inv_diag[k], rhs, precision=highest, preferred_element_type=jnp.float32)
        solutions.append(solution)
        stored = stored + jnp.where(mine, solution, jnp.zeros_like(solution))
    return stored


def solution(mesh):
    split = Mesh(
        mesh.devices.reshape(mesh.shape["row"], 8, 2, 8), ("row", "src_0", "src_1", "src_2")
    )
    return jax.shard_map(
        body,
        mesh=split,
        in_specs=(P(None, None, ROW_SRC), P("row", SRC), P(None, SRC), P(), P(), P()),
        out_specs=P("row", SRC),
        check_vma=False,
    )
```

profile of v0, /device:TPU:6, one launch (start us, length us, event | category | flops | bytes accessed | tf_op | source)
XLA Modules:
  0.0 319.9 jit_solution(6705558419649976911)
XLA Ops:
  6.5 5.1 %all-gather = f32[6,256,16]{1,2,0:T(8,128)S(1)} all-gather(f32[3,256,16]{1,2,0:T(8,128)} %param.6), channel_id=2, replica_groups=mesh['row'=8,'src_0'=8,'src_1'=2,'src_2'=8] {'src_1'}, dimensions={0}, use_global_device_ids=true | all-gather | bytes 147456 | tf_op jit(solution)/shard_map/all_gather | solution.py:20
  11.6 40.5 %all_gather.10 = f32[16,3,256,16]{2,3,1,0:T(8,128)} all-gather(f32[2,3,256,16]{2,3,1,0:T(8,128)S(1)} %bitcast.60), channel_id=1, replica_groups=mesh['row'=8,'src_0'=8,'src_1'=2,'src_2'=8] {'src_0'}, dimensions={0}, use_global_device_ids=true | all-gather | bytes 884736 | tf_op jit(solution)/shard_map/all_gather | solution.py:20
  52.1 0.0 all-gather.3.cloned.1.call-update
  52.1 77.9 %all-gather.3.cloned.1.call-done = f32[128,3,256,16]{2,3,1,0:T(8,128)} async-done(((f32[16,3,256,16]{2,3,1,0:T(8,128)}), f32[128,3,256,16]{2,3,1,0:T(8,128)}) %all-gather.3.cloned.1.call-update) | async-done | bytes 6291472 | tf_op jit(solution)/shard_map/all_gather | solution.py:20
  130.0 3.5 %copy.45 = f32[8,2,8,3,256,16]{4,5,3,2,1,0:T(8,128)S(1)} copy(f32[8,2,8,3,256,16]{4,5,3,1,0,2:T(8,128)} %bitcast.57) | data formatting | bytes 12582912 | tf_op jit(solution)/shard_map/transpose | solution.py:24
  133.5 0.9 copy.46
  134.5 10.2 %fusion = f32[3,256,256]{2,1,0:T(8,128)S(1)} fusion(f32[3,256,2048]{1,2,0:T(8,128)S(1)} %bitcast.56, f32[2048,256]{1,0:T(8,128)S(1)} %copy-done), kind=kOutput, calls=%fused_computation | convolution fusion | flops 4831838208 | bytes 9175040 | tf_op jit(solution)/shard_map/kbn,ns->kbs/dot_general | solution.py:49
  144.7 3.5 %broadcast_in_dim.10 = f32[8,3,256,256]{3,2,1,0:T(8,128)} broadcast(f32[3,256,256]{2,1,0:T(8,128)S(1)} %fusion), dimensions={1,2,3} | broadcast | bytes 7077888 | tf_op jit(solution)/shard_map/broadcast_in_dim | solution.py:34
  148.2 7.0 %all-to-all-start = ((f32[8,3,256,256]{3,2,1,0:T(8,128)}), f32[8,3,256,256]{3,2,1,0:T(8,128)}, u32[]{:S(2)}, u32[]{:S(2)}) async-start(f32[8,3,256,256]{3,2,1,0:T(8,128)} %broadcast_in_dim.10), calls=%async_computation | async-start | bytes 12582912 | tf_op jit(solution)/shard_map/all_to_all | solution.py:33
  155.2 0.8 copy.58
  156.1 0.1 copy.60
  156.2 0.6 fusion.24
  158.5 138.1 %all-to-all-done = f32[8,3,256,256]{3,2,1,0:T(8,128)} async-done(((f32[8,3,256,256]{3,2,1,0:T(8,128)}), f32[8,3,256,256]{3,2,1,0:T(8,128)}, u32[]{:S(2)}, u32[]{:S(2)}) %all-to-all-start) | async-done | bytes 6291488 | tf_op jit(solution)/shard_map/all_to_all | solution.py:33
  296.7 3.3 %reduce_sum.9 = f32[3,256,256]{2,1,0:T(8,128)S(1)} reduce(f32[8,3,256,256]{3,2,1,0:T(8,128)} %all-to-all-done, f32[]{:T(128)} %constant.3.clone.1), dimensions={0}, to_apply=%region_0.0 | reduce | flops 1376256 | bytes 7077892 | tf_op jit(solution)/shard_map/reduce_sum | solution.py:39
  299.9 0.7 fusion.22
  300.7 0.8 copy.59
  301.5 1.4 fusion.11
  303.0 1.7 fusion.4
  304.7 1.4 convolution_bitcast_fusion.1
  306.0 1.1 copy.61
  307.1 0.8 copy.48
  308.0 0.8 copy.52
  308.8 2.0 fusion.5
  310.9 2.2 fusion.3
  (9 shorter events, 0.1 us)
Async XLA Ops:
  6.5 128.0 %copy-start = (f32[2048,256]{1,0:T(8,128)S(1)}, f32[2048,256]{1,0:T(8,128)}, u32[]{:S(2)}) copy-start(f32[2048,256]{1,0:T(8,128)} %param.7) | copy-start | bytes 6291460
  6.5 123.5 %all-gather.3.cloned.1.call-start = ((), (), s32[]{:S(2)}) async-start(), calls=%async_computation.1 | async-start | bytes 7077888 | tf_op jit(solution)/shard_map/all_gather | solution.py:20
  148.2 7.0 %copy-start.1 = (f32[768,256]{1,0:T(8,128)S(1)}, f32[768,256]{1,0:T(8,128)}, u32[]{:S(2)}) copy-start(f32[768,256]{1,0:T(8,128)} %param.8) | copy-start | bytes 2359300
  148.2 8.0 %copy-start.2 = (s32[3]{0:T(128)S(1)}, s32[3]{0:T(128)}, u32[]{:S(2)}) copy-start(s32[3]{0:T(128)} %param.11) | copy-start | bytes 40
  148.2 148.4 %all-to-all-start = ((f32[8,3,256,256]{3,2,1,0:T(8,128)}), f32[8,3,256,256]{3,2,1,0:T(8,128)}, u32[]{:S(2)}, u32[]{:S(2)}) async-start(f32[8,3,256,256]{3,2,1,0:T(8,128)} %broadcast_in_dim.10), calls=%async_computation | async-start | bytes 12582912 | tf_op jit(solution)/shard_map/all_to_all | solution.py:33
Sparse Core Ops, SparseCore 0:
  52.3 77.7 all-gather.2
where the time goes:
time: 321 us; the launch traced here: 320 us
  waiting for transfers between devices  216 us (67%)
  blocking collectives  45.6 us (14%)
  matrix products  18.9 us (6%)
  between operations  15.2 us (5%)
  local copies, waits for them, and re-layouts  13.8 us (4%)
  starting transfers between devices  6.96 us (2%)
  other arithmetic  3.31 us (1%)
    all_to_all x1, waiting for transfers between devices, copy_for_each(): lax.all_to_all(jnp.broadcast_to(shard[None], (peers, *shard.shape)), axis...  138 us
    all_gather x1, waiting for transfers between devices, all_blocks(): pieces = lax.all_gather(pieces, axes[k], axis=0, tiled=True)  77.9 us
    all_gather x2, blocking collectives, all_blocks(): pieces = lax.all_gather(pieces, axes[k], axis=0, tiled=True)  45.6 us
    dot_general x1, matrix products, body(): jnp.einsum('kbn,ns->kbs', panel_rows, solved_prev, precision=highest, pre...  10.2 us
    all_to_all x1, starting transfers between devices, copy_for_each(): lax.all_to_all(jnp.broadcast_to(shard[None], (peers, *shard.shape)), axis...  6.96 us
  transfers between devices with their start and end apart: 2, of which 2 were waited for; matrix products, arithmetic and copies ran while one was open for 0% of the time, Pallas kernels for 0%

commit v1 on v0

v1 whole, which is shorter than its diff:
```python
import jax
import jax.numpy as jnp
from jax import lax
from jax.sharding import Mesh
from jax.sharding import PartitionSpec as P


ROW = ("y_hi", "core")
SRC = ("z", "y_lo", "x")
HIGH = lax.Precision.HIGH
HIGHEST = lax.Precision.HIGHEST
CHUNKS = ((0, 2), (2, 3))


def dot(a, b, dims, precision):
    return lax.dot_general(
        a, b, (dims, ((), ())), precision=precision, preferred_element_type=jnp.float32
    )


def swapped(value, axis):
    return lax.ppermute(value, axis, [(0, 1), (1, 0)])


def in_order(mine, other, axis, dim):
    first = lax.axis_index(axis) == 0
    return jnp.stack([jnp.where(first, mine, other), jnp.where(first, other, mine)], axis=dim)


def body(front_panel, solved_prev, right_side, front_window, inv_diag, owner_map):
    nblk, block, own = front_panel.shape
    _, width = solved_prev.shape
    nz, ny, nx = (lax.axis_size(axis) for axis in SRC)
    nhi, ncore = (lax.axis_size(axis) for axis in ROW)
    groups = nhi * ncore
    part = width // groups
    here = lax.axis_index(ROW)
    y = lax.axis_index("y_lo")
    core = lax.axis_index("core")
    depth = nz * nx * own

    rows_of = solved_prev.reshape(nz, ny, nx * own, width)
    far = lax.dynamic_index_in_dim(rows_of, ny - 1 - y, 1, keepdims=False)
    got = swapped(far, "y_lo")
    near = lax.dynamic_index_in_dim(rows_of, y, 1, keepdims=False)

    panel = front_panel.transpose(2, 0, 1).reshape(own, nblk * block)
    panels, column = [], None
    for first, last in CHUNKS:
        piece = panel[:, first * block : last * block]
        if column is not None:
            piece, column = lax.optimization_barrier((piece, column))
        copies = jnp.broadcast_to(piece[None], (nx, *piece.shape))
        column = lax.all_to_all(copies, "x", 0, 0, tiled=True)
        panels.append(lax.all_gather(column.reshape(nx * own, -1), "z", axis=0, tiled=True))

    sources = in_order(near, got, "y_lo", 0).reshape(ny, depth, width).transpose(0, 2, 1)
    sources = sources.reshape(ny, nhi, ncore, part, depth)
    kept, given = (
        lax.dynamic_index_in_dim(sources, which, 2, keepdims=False)
        .transpose(1, 0, 2, 3)
        .reshape(nhi * ny * part, depth)
        for which in (core, ncore - 1 - core)
    )
    sides = lax.dynamic_slice_in_dim(right_side, here * part, part, axis=1).T

    slots = jnp.arange(groups, dtype=owner_map.dtype)[:, None, None]
    routed = jnp.zeros((groups, part, block), jnp.float32)
    solutions = []
    for (first, last), gathered in zip(CHUNKS, panels):
        others = dot(given, gathered, ((1,), (0,)), HIGH)
        arrived = swapped(others, "core")
        local = lax.optimization_barrier(dot(kept, gathered, ((1,), (0,)), HIGH))
        local = local + arrived
        pieces = lax.all_to_all(
            local.reshape(nhi * ny, part, -1), ("y_hi", "y_lo"), 0, 0, tiled=True
        )
        rest = sides[:, first * block : last * block] - pieces.sum(axis=0)
        for k in range(first, last):
            rhs = rest[:, (k - first) * block : (k - first + 1) * block]
            for j, earlier in enumerate(solutions):
                window = front_window[k * block : (k + 1) * block, j * block : (j + 1) * block]
                rhs = rhs - dot(earlier, window, ((1,), (1,)), HIGHEST)
            solution_k = dot(rhs, inv_diag[k], ((1,), (1,)), HIGHEST)
            solutions.append(solution_k)
            routed = jnp.where(slots == owner_map[k], solution_k[None], routed)
    stored = lax.all_to_all(routed, ROW, 0, 0, tiled=True)
    return stored.reshape(width, block).T


def solution(mesh):
    split = Mesh(
        mesh.devices.reshape(mesh.shape["row"] // 2, 2, 8, 2, 8), ("y_hi", "core", "z", "y_lo", "x")
    )
    return jax.shard_map(
        body,
        mesh=split,
        in_specs=(P(None, None, (*ROW, *SRC)), P(ROW, SRC), P(None, SRC), P(), P(), P()),
        out_specs=P(ROW, SRC),
        check_vma=False,
    )
```

time: 321 us -> 215 us (0.67)
  the two profiles are of different devices: /device:TPU:6 before, /device:TPU:2 now
where the time goes in v1:
time: 215 us
  waiting for transfers between devices  109 us (51%)
  starting transfers between devices  32.6 us (15%)
  blocking collectives  27.5 us (13%)
  between operations  13.7 us (6%)
  matrix products  13.5 us (6%)
  local copies, waits for them, and re-layouts  9.91 us (5%)
  other arithmetic  8.4 us (4%)
    all_gather x2, waiting for transfers between devices, body(): lax.all_gather(column.reshape(nx * own, -1), 'z', axis=0, tiled=True)  60.3 us
    all_to_all x2, waiting for transfers between devices, body(): lax.all_to_all(local.reshape(nhi * ny, part, -1), ('y_hi', 'y_lo'), 0, 0,...  23.9 us
    all_to_all x1, starting transfers between devices, body(): column = lax.all_to_all(copies, 'x', 0, 0, tiled=True)  16.5 us
    ppermute x3, waiting for transfers between devices, swapped(): return lax.ppermute(value, axis, [(0, 1), (1, 0)])  14.7 us
    all_to_all x1, blocking collectives, body(): stored = lax.all_to_all(routed, ROW, 0, 0, tiled=True)  14.5 us
    dot_general x10, matrix products, dot(): lax.dot_general(a, b, (dims, ((), ())), precision=precision, preferred_el...  13.5 us
    all_to_all x1, blocking collectives, body(): column = lax.all_to_all(copies, 'x', 0, 0, tiled=True)  13.1 us
    all_to_all x2, starting transfers between devices, body(): lax.all_to_all(local.reshape(nhi * ny, part, -1), ('y_hi', 'y_lo'), 0, 0,...  10.3 us
  transfers between devices with their start and end apart: 8, of which 6 were waited for; matrix products, arithmetic and copies ran while one was open for 11% of the time, Pallas kernels for 0%

profile of v1, /device:TPU:2, one launch (start us, length us, event | category | flops | bytes accessed | tf_op | source)
XLA Modules:
  0.0 214.6 jit_solution(7295924543275569397)
XLA Ops:
  8.2 16.5 %all-to-all-start = ((f32[8,16,512]{2,1,0:T(8,128)}), f32[8,16,512]{2,1,0:T(8,128)S(1)}, u32[]{:S(2)}, u32[]{:S(2)}) async-start(f32[8,16,512]{2,1,0:T(8,128)} %broadcast_in_dim.56), calls=%async_computation | async-start | bytes 524288 | tf_op jit(solution)/shard_map/all_to_all | solution.py:54
  24.6 9.3 %all-to-all-done = f32[8,16,512]{2,1,0:T(8,128)S(1)} async-done(((f32[8,16,512]{2,1,0:T(8,128)}), f32[8,16,512]{2,1,0:T(8,128)S(1)}, u32[]{:S(2)}, u32[]{:S(2)}) %all-to-all-start) | async-done | bytes 262176 | tf_op jit(solution)/shard_map/all_to_all | solution.py:54
  34.0 13.1 %all_to_all.25 = f32[8,16,256]{2,1,0:T(8,128)} all-to-all(f32[8,16,256]{2,1,0:T(8,128)S(1)} %broadcast_in_dim.57), channel_id=1, replica_groups=mesh['y_hi'=4,'core'=2,'z'=8,'y_lo'=2,'x'=8] {'x'}, dimensions={0} | all-to-all | bytes 262144 | tf_op jit(solution)/shard_map/all_to_all | solution.py:54
  47.8 1.8 constant_dynamic-slice_fusion.1
  49.6 1.3 copy.16
  50.9 1.9 collective-permute-start
  53.3 14.7 %collective-permute-done = f32[8,128,256]{1,0,2:T(8,128)} collective-permute-done((f32[8,128,256]{1,0,2:T(8,128)}, f32[8,128,256]{1,0,2:T(8,128)}, u32[]{:S(2)}, u32[]{:S(2)}) %collective-permute-start) | collective-permute-done | bytes 1048608 | tf_op jit(solution)/shard_map/ppermute | solution.py:22
  67.9 2.3 %bitcast_select_fusion.1 = (f32[8,128,256]{1,0,2:T(8,128)S(1)}, f32[8,128,256]{1,0,2:T(8,128)}) fusion(f32[8,128,256]{1,0,2:T(8,128)} %collective-permute-done, f32[8,1,128,256]{2,0,3,1:T(8,128)S(1)} %copy.15, pred[]{:T(512)S(6)} %eq.38), kind=kLoop, calls=%fused_computation.4 | loop fusion | flops 524288 | bytes 4194305 | tf_op jit(solution)/shard_map/jit(_where)/select_n | solution.py:27
  70.2 1.4 stack.10
  72.8 1.4 pad_maximum_fusion
  74.7 16.4 %all-gather.3.cloned.1.call-done = f32[1024,256]{1,0:T(8,128)} async-done(((f32[128,256]{1,0:T(8,128)}), f32[1024,256]{1,0:T(8,128)}) %all-gather.3.cloned.1.call-update) | async-done | bytes 1048592 | tf_op jit(solution)/shard_map/all_gather | solution.py:55
  91.1 2.5 %fusion.17 = f32[256,256]{1,0:T(8,128)} fusion(f32[256,1024]{1,0:T(8,128)S(1)} %bitcast.60, f32[1024,256]{1,0:T(8,128)} %all-gather.3.cloned.1.call-done), kind=kOutput, calls=%fused_computation.33 | convolution fusion | flops 402653184 | bytes 2359296 | tf_op jit(solution)/shard_map/dot_general | solution.py:16
  93.7 1.9 collective-permute-start.1
  95.6 43.9 %all-gather.5.cloned.1.call-done = f32[1024,512]{1,0:T(8,128)} async-done(((f32[128,512]{1,0:T(8,128)}), f32[1024,512]{1,0:T(8,128)}) %all-gather.5.cloned.1.call-update) | async-done | bytes 2097168 | tf_op jit(solution)/shard_map/all_gather | solution.py:55
  139.5 2.8 %fusion.19 = f32[256,512]{1,0:T(8,128)S(1)} fusion(f32[256,1024]{1,0:T(8,128)S(1)} %bitcast.61, f32[1024,512]{1,0:T(8,128)} %all-gather.5.cloned.1.call-done), kind=kOutput, calls=%fused_computation.35 | convolution fusion | flops 805306368 | bytes 3670016 | tf_op jit(solution)/shard_map/dot_general | solution.py:16
  142.2 1.9 collective-permute-start.2
  144.8 1.7 add.34
  146.5 6.8 %all-to-all-start.2 = ((f32[8,32,256]{2,1,0:T(8,128)}), f32[8,32,256]{2,1,0:T(8,128)S(1)}, u32[]{:S(2)}, u32[]{:S(2)}) async-start(f32[8,32,256]{2,1,0:T(8,128)} %bitcast.16), calls=%async_computation.2 | async-start | bytes 524288 | tf_op jit(solution)/shard_map/all_to_all | solution.py:75
  153.3 2.7 %fusion.18 = f32[256,512]{1,0:T(8,128)S(1)} fusion(f32[256,1024]{1,0:T(8,128)S(1)} %bitcast.59, f32[1024,512]{1,0:T(8,128)} %all-gather.5.cloned.1.call-done), kind=kOutput, calls=%fused_computation.34 | convolution fusion | flops 805306368 | bytes 3670016 | tf_op jit(solution)/shard_map/dot_general | solution.py:16
  156.9 8.9 %all-to-all-done.2 = f32[8,32,256]{2,1,0:T(8,128)S(1)} async-done(((f32[8,32,256]{2,1,0:T(8,128)}), f32[8,32,256]{2,1,0:T(8,128)S(1)}, u32[]{:S(2)}, u32[]{:S(2)}) %all-to-all-start.2) | async-done | bytes 262176 | tf_op jit(solution)/shard_map/all_to_all | solution.py:75
  165.9 3.5 %all-to-all-start.3 = ((f32[8,32,512]{2,1,0:T(8,128)}), f32[8,32,512]{2,1,0:T(8,128)S(1)}, u32[]{:S(2)}, u32[]{:S(2)}) async-start(f32[8,32,512]{2,1,0:T(8,128)} %bitcast.18), calls=%async_computation.3 | async-start | bytes 1048576 | tf_op jit(solution)/shard_map/all_to_all | solution.py:75
  172.3 15.0 %all-to-all-done.3 = f32[8,32,512]{2,1,0:T(8,128)S(1)} async-done(((f32[8,32,512]{2,1,0:T(8,128)}), f32[8,32,512]{2,1,0:T(8,128)S(1)}, u32[]{:S(2)}, u32[]{:S(2)}) %all-to-all-start.3) | async-done | bytes 524320 | tf_op jit(solution)/shard_map/all_to_all | solution.py:75
  187.7 1.3 convolution_subtract_fusion.1
  192.4 14.5 %all_to_all.26 = f32[8,32,256]{2,1,0:T(8,128)S(1)} all-to-all(f32[8,32,256]{2,1,0:T(8,128)S(1)} %select_select_fusion), channel_id=1, replica_groups=mesh['y_hi'=4,'core'=2,'z'=8,'y_lo'=2,'x'=8] {'y_hi','core'}, dimensions={0} | all-to-all | bytes 524288 | tf_op jit(solution)/shard_map/all_to_all | solution.py:87
  (43 shorter events, 13.4 us)
Async XLA Ops:
  6.5 162.9 %copy-start = (f32[768,256]{1,0:T(8,128)S(1)}, f32[768,256]{1,0:T(8,128)}, u32[]{:S(2)}) copy-start(f32[768,256]{1,0:T(8,128)} %param.8) | copy-start | bytes 2359300
  8.2 25.8 %all-to-all-start = ((f32[8,16,512]{2,1,0:T(8,128)}), f32[8,16,512]{2,1,0:T(8,128)S(1)}, u32[]{:S(2)}, u32[]{:S(2)}) async-start(f32[8,16,512]{2,1,0:T(8,128)} %broadcast_in_dim.56), calls=%async_computation | async-start | bytes 524288 | tf_op jit(solution)/shard_map/all_to_all | solution.py:54
  24.6 66.5 %all-gather.3.cloned.1.call-start = ((), (), s32[]{:S(2)}) async-start(), calls=%async_computation.5 | async-start | bytes 1179648 | tf_op jit(solution)/shard_map/all_gather | solution.py:55
  34.0 13.2 %copy-start.2 = (f32[8,16,512]{2,1,0:T(8,128)}, f32[8,16,512]{2,1,0:T(8,128)S(1)}, u32[]{:S(2)}) copy-start(f32[8,16,512]{2,1,0:T(8,128)S(1)} %all-to-all-done) | copy-start | bytes 786436
  47.1 92.4 %all-gather.5.cloned.1.call-start = ((), (), s32[]{:S(2)}) async-start(), calls=%async_computation.6 | async-start | bytes 2359296 | tf_op jit(solution)/shard_map/all_gather | solution.py:55
  50.9 17.0 %collective-permute-start = (f32[8,128,256]{1,0,2:T(8,128)}, f32[8,128,256]{1,0,2:T(8,128)}, u32[]{:S(2)}, u32[]{:S(2)}) collective-permute-start(f32[8,128,256]{1,0,2:T(8,128)} %bitcast.64), channel_id=1, source_target_pairs={{0,8},{8,0},{1,9},{9,1},{2,10},{10,2},{3,11},{11,3},{4,12},{12,4},... | collective-permute-start | bytes 3145736 | tf_op jit(solution)/shard_map/ppermute | solution.py:22
  93.7 51.1 %collective-permute-start.1 = (f32[256,256]{1,0:T(8,128)}, f32[256,256]{1,0:T(8,128)}, u32[]{:S(2)}, u32[]{:S(2)}) collective-permute-start(f32[256,256]{1,0:T(8,128)} %fusion.17), channel_id=1, source_target_pairs={{0,128},{128,0},{1,129},{129,1},{2,130},{130,2},{3,131},{131,3},{4... | collective-permute-start | bytes 786440 | tf_op jit(solution)/shard_map/ppermute | solution.py:22
  139.5 4.7 %copy-start.1 = (f32[1024,256]{1,0:T(8,128)S(1)}, f32[1024,256]{1,0:T(8,128)}, u32[]{:S(2)}) copy-start(f32[1024,256]{1,0:T(8,128)} %all-gather.3.cloned.1.call-done) | copy-start | bytes 3145732
  142.2 13.8 %collective-permute-start.2 = (f32[256,512]{1,0:T(8,128)S(1)}, f32[256,512]{1,0:T(8,128)S(1)}, u32[]{:S(2)}, u32[]{:S(2)}) collective-permute-start(f32[256,512]{1,0:T(8,128)S(1)} %fusion.19), channel_id=1, source_target_pairs={{0,128},{128,0},{1,129},{129,1},{2,130},{130,2},{3,131},{131,3},{4... | collective-permute-start | bytes 1572872 | tf_op jit(solution)/shard_map/ppermute | solution.py:22
  146.5 19.4 %all-to-all-start.2 = ((f32[8,32,256]{2,1,0:T(8,128)}), f32[8,32,256]{2,1,0:T(8,128)S(1)}, u32[]{:S(2)}, u32[]{:S(2)}) async-start(f32[8,32,256]{2,1,0:T(8,128)} %bitcast.16), calls=%async_computation.2 | async-start | bytes 524288 | tf_op jit(solution)/shard_map/all_to_all | solution.py:75
  156.0 13.7 %copy-start.4 = (s32[3]{0:T(128)S(1)}, s32[3]{0:T(128)}, u32[]{:S(2)}) copy-start(s32[3]{0:T(128)} %param.11) | copy-start | bytes 40
  156.9 30.4 %copy-start.3 = (f32[3,256,256]{2,1,0:T(8,128)S(1)}, f32[3,256,256]{2,1,0:T(8,128)}, u32[]{:S(2)}) copy-start(f32[3,256,256]{2,1,0:T(8,128)} %param.10) | copy-start | bytes 2359300
  165.9 21.4 %all-to-all-start.3 = ((f32[8,32,512]{2,1,0:T(8,128)}), f32[8,32,512]{2,1,0:T(8,128)S(1)}, u32[]{:S(2)}, u32[]{:S(2)}) async-start(f32[8,32,512]{2,1,0:T(8,128)} %bitcast.18), calls=%async_computation.3 | async-start | bytes 1048576 | tf_op jit(solution)/shard_map/all_to_all | solution.py:75
Sparse Core Ops, SparseCore 0:
  47.2 43.8 all-gather.2
  93.8 45.6 all-gather.4

commit v2 on v1

v2 whole, which is shorter than its diff:
```python
import jax
import jax.numpy as jnp
from jax import lax
from jax.sharding import Mesh
from jax.sharding import PartitionSpec as P


ROW = ("y_hi", "core")
SRC = ("z", "y_lo", "x")
HIGH = lax.Precision.HIGH
HIGHEST = lax.Precision.HIGHEST


def dot(a, b, dims, precision):
    return lax.dot_general(
        a, b, (dims, ((), ())), precision=precision, preferred_element_type=jnp.float32
    )


def swapped(value, axis):
    return lax.ppermute(value, axis, [(0, 1), (1, 0)])


def passed_on(value, axis, step):
    n = lax.axis_size(axis)
    return lax.ppermute(value, axis, [(i, (i + step) % n) for i in range(n)])


def ring(rows, axis):
    n = lax.axis_size(axis)
    half = rows.shape[0] // 2
    up = down = rows
    yield 0, 0, rows
    for step in range(1, n // 2):
        up, down = passed_on(up, axis, 1), passed_on(down, axis, -1)
        yield -step, 0, up
        yield step, 0, down
    yield n // 2, 0, passed_on(up[:half], axis, 1)
    yield n // 2, half, passed_on(down[half:], axis, -1)


def in_order(mine, other, axis, dim):
    first = lax.axis_index(axis) == 0
    return jnp.stack([jnp.where(first, mine, other), jnp.where(first, other, mine)], axis=dim)


def body(front_panel, solved_prev, right_side, front_window, inv_diag, owner_map):
    nblk, block, own = front_panel.shape
    _, width = solved_prev.shape
    nz, ny, nx = (lax.axis_size(axis) for axis in SRC)
    nhi, ncore = (lax.axis_size(axis) for axis in ROW)
    groups = nhi * ncore
    part = width // groups
    here = lax.axis_index(ROW)
    y = lax.axis_index("y_lo")
    core = lax.axis_index("core")

    rows_of = solved_prev.reshape(nz, ny, nx * own, width)
    far = lax.dynamic_index_in_dim(rows_of, ny - 1 - y, 1, keepdims=False)
    got = swapped(far, "y_lo")
    near = lax.dynamic_index_in_dim(rows_of, y, 1, keepdims=False)

    panel = front_panel.transpose(2, 0, 1).reshape(own, nblk * block)
    column = lax.all_to_all(
        jnp.broadcast_to(panel[None], (nx, *panel.shape)), "x", 0, 0, tiled=True
    )
    column = column.reshape(nx * own, nblk * block)

    sources = in_order(near, got, "y_lo", 0).reshape(ny, nz, nx * own, width).transpose(1, 0, 3, 2)
    sources = sources.reshape(nz, ny, nhi, ncore, part, nx * own)
    kept, given = (
        lax.dynamic_index_in_dim(sources, which, 3, keepdims=False)
        .transpose(0, 2, 1, 3, 4)
        .reshape(nz, nhi * ny * part, nx * own)
        for which in (core, ncore - 1 - core)
    )
    sides = lax.dynamic_slice_in_dim(right_side, here * part, part, axis=1).T

    local = jnp.zeros((nhi * ny * part, nblk * block), jnp.float32)
    others = local
    for offset, first, rows in ring(column, "z"):
        place = (lax.axis_index("z") + offset) % nz
        span = slice(first, first + rows.shape[0])
        given_rows, kept_rows = (
            lax.dynamic_index_in_dim(held, place, 0, keepdims=False)[:, span]
            for held in (given, kept)
        )
        others += dot(given_rows, rows, ((1,), (0,)), HIGH)
        local += dot(kept_rows, rows, ((1,), (0,)), HIGH)
    local = lax.optimization_barrier(local) + swapped(others, "core")
    pieces = lax.all_to_all(
        local.reshape(nhi * ny, part, nblk * block), ("y_hi", "y_lo"), 0, 0, tiled=True
    )
    rest = sides - pieces.sum(axis=0)

    slots = jnp.arange(groups, dtype=owner_map.dtype)[:, None, None]
    routed = jnp.zeros((groups, part, block), jnp.float32)
    solutions = []
    for k in range(nblk):
        rhs = rest[:, k * block : (k + 1) * block]
        for j, earlier in enumerate(solutions):
            window = front_window[k * block : (k + 1) * block, j * block : (j + 1) * block]
            rhs = rhs - dot(earlier, window, ((1,), (1,)), HIGHEST)
        solution_k = dot(rhs, inv_diag[k], ((1,), (1,)), HIGHEST)
        solutions.append(solution_k)
        routed = jnp.where(slots == owner_map[k], solution_k[None], routed)
    stored = lax.all_to_all(routed, ROW, 0, 0, tiled=True)
    return stored.reshape(width, block).T


def solution(mesh):
    split = Mesh(
        mesh.devices.reshape(mesh.shape["row"] // 2, 2, 8, 2, 8), ("y_hi", "core", "z", "y_lo", "x")
    )
    return jax.shard_map(
        body,
        mesh=split,
        in_specs=(P(None, None, (*ROW, *SRC)), P(ROW, SRC), P(None, SRC), P(), P(), P()),
        out_specs=P(ROW, SRC),
        check_vma=False,
    )
```

time: 215 us -> 150 us (0.70)
  the two profiles are of different devices: /device:TPU:2 before, /device:TPU:1 now
where the time goes in v2:
time: 150 us; the launch traced here: 149 us
  starting transfers between devices  68.5 us (46%)
  waiting for transfers between devices  41.6 us (28%)
  matrix products  13.8 us (9%)
  blocking collectives  13.2 us (9%)
  local copies, waits for them, and re-layouts  6.5 us (4%)
  other arithmetic  4.62 us (3%)
    ppermute x8, starting transfers between devices, passed_on(): return lax.ppermute(value, axis, [(i, (i + step) % n) for i in range(n)])  43.1 us
    all_to_all x1, waiting for transfers between devices, body(): lax.all_to_all(local.reshape(nhi * ny, part, nblk * block), ('y_hi', 'y_l...  20.7 us
    dot_general x24, matrix products, dot(): lax.dot_general(a, b, (dims, ((), ())), precision=precision, preferred_el...  13.8 us
    all_to_all x1, blocking collectives, body(): stored = lax.all_to_all(routed, ROW, 0, 0, tiled=True)  13.2 us
    ppermute x2, starting transfers between devices, swapped(): return lax.ppermute(value, axis, [(0, 1), (1, 0)])  12.4 us
    all_to_all x1, waiting for transfers between devices, body(): lax.all_to_all(jnp.broadcast_to(panel[None], (nx, *panel.shape)), 'x', 0,...  10.4 us
    ppermute x8, waiting for transfers between devices, passed_on(): return lax.ppermute(value, axis, [(i, (i + step) % n) for i in range(n)])  10.2 us
    all_to_all x1, starting transfers between devices, body(): lax.all_to_all(local.reshape(nhi * ny, part, nblk * block), ('y_hi', 'y_l...  6.48 us
  transfers between devices with their start and end apart: 12, of which 8 were waited for; matrix products, arithmetic and copies ran while one was open for 9% of the time, Pallas kernels for 0%

profile of v2, /device:TPU:1, one launch (start us, length us, event | category | flops | bytes accessed | tf_op | source)
XLA Modules:
  0.0 148.7 jit_solution(16122982485375177615)
XLA Ops:
  0.0 1.8 %constant_dynamic-slice_fusion.1 = (f32[8,1,128,256]{3,2,1,0:T(8,128)S(1)}, f32[8,1,128,256]{3,2,1,0:T(8,128)S(1)}) fusion(f32[8,2,128,256]{3,2,1,0:T(8,128)} %bitcast.140, s32[]{:T(128)S(6)} %select_n.113, s32[]{:T(128)S(6)} %select_n.114), kind=kLoop, calls=%fused_computation.100 | loop fusion | bytes 4194312 | tf_op jit(solution)/shard_map/jit(dynamic_index_in_dim)/dynamic_slice | solution.py:61
  1.8 1.3 copy.25
  3.2 4.1 %collective-permute-start = (f32[8,128,256]{1,2,0:T(8,128)}, f32[8,128,256]{1,2,0:T(8,128)}, u32[]{:S(2)}, u32[]{:S(2)}) collective-permute-start(f32[8,128,256]{1,2,0:T(8,128)} %bitcast.141), channel_id=1, source_target_pairs={{0,8},{8,0},{1,9},{9,1},{2,10},{10,2},{3,11},{11,3},{4,12},{12,4},... | collective-permute-start | bytes 3145736 | tf_op jit(solution)/shard_map/ppermute | solution.py:21
  8.1 6.5 %all-to-all-start = ((f32[8,16,768]{2,1,0:T(8,128)}), f32[8,16,768]{2,1,0:T(8,128)S(1)}, u32[]{:S(2)}, u32[]{:S(2)}) async-start(f32[8,16,768]{2,1,0:T(8,128)} %broadcast_in_dim.52), calls=%async_computation | async-start | bytes 786432 | tf_op jit(solution)/shard_map/all_to_all | solution.py:64
  14.9 10.4 %all-to-all-done = f32[8,16,768]{2,1,0:T(8,128)S(1)} async-done(((f32[8,16,768]{2,1,0:T(8,128)}), f32[8,16,768]{2,1,0:T(8,128)S(1)}, u32[]{:S(2)}, u32[]{:S(2)}) %all-to-all-start) | async-done | bytes 393248 | tf_op jit(solution)/shard_map/all_to_all | solution.py:64
  25.3 7.7 %collective-permute-start.1 = (f32[128,768]{1,0:T(8,128)S(1)}, f32[128,768]{1,0:T(8,128)S(1)}, u32[]{:S(2)}, u32[]{:S(2)}) collective-permute-start(f32[128,768]{1,0:T(8,128)S(1)} %bitcast.136), channel_id=1, source_target_pairs={{0,16},{16,32},{32,48},{48,64},{64,80},{80,96},{96,112},{112,0},{1... | collective-permute-start | bytes 1179656 | tf_op jit(solution)/shard_map/ppermute | solution.py:26
  33.0 14.1 %collective-permute-start.2 = (f32[128,768]{1,0:T(8,128)S(1)}, f32[128,768]{1,0:T(8,128)S(1)}, u32[]{:S(2)}, u32[]{:S(2)}) collective-permute-start(f32[128,768]{1,0:T(8,128)S(1)} %bitcast.137), channel_id=1, source_target_pairs={{0,112},{16,0},{32,16},{48,32},{64,48},{80,64},{96,80},{112,96},{1... | collective-permute-start | bytes 1179656 | tf_op jit(solution)/shard_map/ppermute | solution.py:26
  47.1 1.4 fusion.8
  50.1 3.3 %collective-permute-done.2 = f32[128,768]{1,0:T(8,128)S(1)} collective-permute-done((f32[128,768]{1,0:T(8,128)S(1)}, f32[128,768]{1,0:T(8,128)S(1)}, u32[]{:S(2)}, u32[]{:S(2)}) %collective-permute-start.2) | collective-permute-done | bytes 393248 | tf_op jit(solution)/shard_map/ppermute | solution.py:26
  53.4 5.3 %collective-permute-start.4 = (f32[128,768]{1,0:T(8,128)S(1)}, f32[128,768]{1,0:T(8,128)S(1)}, u32[]{:S(2)}, u32[]{:S(2)}) collective-permute-start(f32[128,768]{1,0:T(8,128)S(1)} %collective-permute-done.2), channel_id=1, source_target_pairs={{0,112},{16,0},{32,16},{48,32},{64,48},{80,64},{96,80},{112,96},{1... | collective-permute-start | bytes 1179656 | tf_op jit(solution)/shard_map/ppermute | solution.py:26
  58.7 1.9 %collective-permute-start.3 = (f32[128,768]{1,0:T(8,128)S(1)}, f32[128,768]{1,0:T(8,128)S(1)}, u32[]{:S(2)}, u32[]{:S(2)}) collective-permute-start(f32[128,768]{1,0:T(8,128)S(1)} %collective-permute-done.1), channel_id=1, source_target_pairs={{0,16},{16,32},{32,48},{48,64},{64,80},{80,96},{96,112},{112,0},{1... | collective-permute-start | bytes 1179656 | tf_op jit(solution)/shard_map/ppermute | solution.py:26
  62.6 1.5 %collective-permute-done.4 = f32[128,768]{1,0:T(8,128)S(1)} collective-permute-done((f32[128,768]{1,0:T(8,128)S(1)}, f32[128,768]{1,0:T(8,128)S(1)}, u32[]{:S(2)}, u32[]{:S(2)}) %collective-permute-start.4) | collective-permute-done | bytes 393248 | tf_op jit(solution)/shard_map/ppermute | solution.py:26
  64.2 5.3 %collective-permute-start.6 = (f32[128,768]{1,0:T(8,128)S(1)}, f32[128,768]{1,0:T(8,128)S(1)}, u32[]{:S(2)}, u32[]{:S(2)}) collective-permute-start(f32[128,768]{1,0:T(8,128)S(1)} %collective-permute-done.4), channel_id=1, source_target_pairs={{0,112},{16,0},{32,16},{48,32},{64,48},{80,64},{96,80},{112,96},{1... | collective-permute-start | bytes 1179656 | tf_op jit(solution)/shard_map/ppermute | solution.py:26
  70.0 1.9 %collective-permute-start.5 = (f32[128,768]{1,0:T(8,128)S(1)}, f32[128,768]{1,0:T(8,128)S(1)}, u32[]{:S(2)}, u32[]{:S(2)}) collective-permute-start(f32[128,768]{1,0:T(8,128)S(1)} %collective-permute-done.3), channel_id=1, source_target_pairs={{0,16},{16,32},{32,48},{48,64},{64,80},{80,96},{96,112},{112,0},{1... | collective-permute-start | bytes 1179656 | tf_op jit(solution)/shard_map/ppermute | solution.py:26
  74.2 5.0 %collective-permute-start.8 = (f32[64,768]{1,0:T(8,128)S(1)}, f32[64,768]{1,0:T(8,128)S(1)}, u32[]{:S(2)}, u32[]{:S(2)}) collective-permute-start(f32[64,768]{1,0:T(8,128)S(1)} %slice.75), channel_id=1, source_target_pairs={{0,112},{16,0},{32,16},{48,32},{64,48},{80,64},{96,80},{112,96},{1... | collective-permute-start | bytes 589832 | tf_op jit(solution)/shard_map/ppermute | solution.py:26
  79.7 1.9 %collective-permute-start.7 = (f32[64,768]{1,0:T(8,128)S(1)}, f32[64,768]{1,0:T(8,128)S(1)}, u32[]{:S(2)}, u32[]{:S(2)}) collective-permute-start(f32[64,768]{1,0:T(8,128)S(1)} %slice.73), channel_id=1, source_target_pairs={{0,16},{16,32},{32,48},{48,64},{64,80},{80,96},{96,112},{112,0},{1... | collective-permute-start | bytes 589832 | tf_op jit(solution)/shard_map/ppermute | solution.py:26
  83.2 4.2 %collective-permute-done.7 = f32[64,768]{1,0:T(8,128)S(1)} collective-permute-done((f32[64,768]{1,0:T(8,128)S(1)}, f32[64,768]{1,0:T(8,128)S(1)}, u32[]{:S(2)}, u32[]{:S(2)}) %collective-permute-start.7) | collective-permute-done | bytes 196640 | tf_op jit(solution)/shard_map/ppermute | solution.py:26
  88.4 8.3 %collective-permute-start.9 = (f32[256,768]{1,0:T(8,128)S(1)}, f32[256,768]{1,0:T(8,128)S(1)}, u32[]{:S(2)}, u32[]{:S(2)}) collective-permute-start(f32[256,768]{1,0:T(8,128)S(1)} %fusion.2), channel_id=1, source_target_pairs={{0,128},{128,0},{1,129},{129,1},{2,130},{130,2},{3,131},{131,3},{4... | collective-permute-start | bytes 2359304 | tf_op jit(solution)/shard_map/ppermute | solution.py:21
  99.5 6.5 %all-to-all-start.1 = ((f32[8,32,768]{2,1,0:T(8,128)}), f32[8,32,768]{2,1,0:T(8,128)S(1)}, u32[]{:S(2)}, u32[]{:S(2)}) async-start(f32[8,32,768]{2,1,0:T(8,128)} %bitcast.35), calls=%async_computation.1 | async-start | bytes 1572864 | tf_op jit(solution)/shard_map/all_to_all | solution.py:91
  108.9 20.7 %all-to-all-done.1 = f32[8,32,768]{2,1,0:T(8,128)S(1)} async-done(((f32[8,32,768]{2,1,0:T(8,128)}), f32[8,32,768]{2,1,0:T(8,128)S(1)}, u32[]{:S(2)}, u32[]{:S(2)}) %all-to-all-start.1) | async-done | bytes 786464 | tf_op jit(solution)/shard_map/all_to_all | solution.py:91
  130.0 1.3 convolution_subtract_fusion.2
  131.3 1.3 convolution_subtract_fusion.1
  133.0 1.3 convolution_subtract_fusion
  134.7 13.2 %all_to_all.15 = f32[8,32,256]{2,1,0:T(8,128)S(1)} all-to-all(f32[8,32,256]{2,1,0:T(8,128)S(1)} %select_select_fusion), channel_id=1, replica_groups=mesh['y_hi'=4,'core'=2,'z'=8,'y_lo'=2,'x'=8] {'y_hi','core'}, dimensions={0} | all-to-all | bytes 524288 | tf_op jit(solution)/shard_map/all_to_all | solution.py:107
  (56 shorter events, 18.1 us)
Async XLA Ops:
  0.0 106.0 %copy-start = (f32[768,256]{1,0:T(8,128)S(1)}, f32[768,256]{1,0:T(8,128)}, u32[]{:S(2)}) copy-start(f32[768,256]{1,0:T(8,128)} %param.8) | copy-start | bytes 2359300
  0.0 7.3 %copy-start.2 = (f32[3,256,16]{1,2,0:T(8,128)S(1)}, f32[3,256,16]{1,2,0:T(8,128)}, u32[]{:S(2)}) copy-start(f32[3,256,16]{1,2,0:T(8,128)} %param.6) | copy-start | bytes 147460
  3.2 43.9 %collective-permute-start = (f32[8,128,256]{1,2,0:T(8,128)}, f32[8,128,256]{1,2,0:T(8,128)}, u32[]{:S(2)}, u32[]{:S(2)}) collective-permute-start(f32[8,128,256]{1,2,0:T(8,128)} %bitcast.141), channel_id=1, source_target_pairs={{0,8},{8,0},{1,9},{9,1},{2,10},{10,2},{3,11},{11,3},{4,12},{12,4},... | collective-permute-start | bytes 3145736 | tf_op jit(solution)/shard_map/ppermute | solution.py:21
  8.1 17.2 %all-to-all-start = ((f32[8,16,768]{2,1,0:T(8,128)}), f32[8,16,768]{2,1,0:T(8,128)S(1)}, u32[]{:S(2)}, u32[]{:S(2)}) async-start(f32[8,16,768]{2,1,0:T(8,128)} %broadcast_in_dim.52), calls=%async_computation | async-start | bytes 786432 | tf_op jit(solution)/shard_map/all_to_all | solution.py:64
  25.3 33.4 %collective-permute-start.1 = (f32[128,768]{1,0:T(8,128)S(1)}, f32[128,768]{1,0:T(8,128)S(1)}, u32[]{:S(2)}, u32[]{:S(2)}) collective-permute-start(f32[128,768]{1,0:T(8,128)S(1)} %bitcast.136), channel_id=1, source_target_pairs={{0,16},{16,32},{32,48},{48,64},{64,80},{80,96},{96,112},{112,0},{1... | collective-permute-start | bytes 1179656 | tf_op jit(solution)/shard_map/ppermute | solution.py:26
  33.0 20.4 %collective-permute-start.2 = (f32[128,768]{1,0:T(8,128)S(1)}, f32[128,768]{1,0:T(8,128)S(1)}, u32[]{:S(2)}, u32[]{:S(2)}) collective-permute-start(f32[128,768]{1,0:T(8,128)S(1)} %bitcast.137), channel_id=1, source_target_pairs={{0,112},{16,0},{32,16},{48,32},{64,48},{80,64},{96,80},{112,96},{1... | collective-permute-start | bytes 1179656 | tf_op jit(solution)/shard_map/ppermute | solution.py:26
  53.4 10.8 %collective-permute-start.4 = (f32[128,768]{1,0:T(8,128)S(1)}, f32[128,768]{1,0:T(8,128)S(1)}, u32[]{:S(2)}, u32[]{:S(2)}) collective-permute-start(f32[128,768]{1,0:T(8,128)S(1)} %collective-permute-done.2), channel_id=1, source_target_pairs={{0,112},{16,0},{32,16},{48,32},{64,48},{80,64},{96,80},{112,96},{1... | collective-permute-start | bytes 1179656 | tf_op jit(solution)/shard_map/ppermute | solution.py:26
  58.7 11.3 %collective-permute-start.3 = (f32[128,768]{1,0:T(8,128)S(1)}, f32[128,768]{1,0:T(8,128)S(1)}, u32[]{:S(2)}, u32[]{:S(2)}) collective-permute-start(f32[128,768]{1,0:T(8,128)S(1)} %collective-permute-done.1), channel_id=1, source_target_pairs={{0,16},{16,32},{32,48},{48,64},{64,80},{80,96},{96,112},{112,0},{1... | collective-permute-start | bytes 1179656 | tf_op jit(solution)/shard_map/ppermute | solution.py:26
  64.2 10.0 %collective-permute-start.6 = (f32[128,768]{1,0:T(8,128)S(1)}, f32[128,768]{1,0:T(8,128)S(1)}, u32[]{:S(2)}, u32[]{:S(2)}) collective-permute-start(f32[128,768]{1,0:T(8,128)S(1)} %collective-permute-done.4), channel_id=1, source_target_pairs={{0,112},{16,0},{32,16},{48,32},{64,48},{80,64},{96,80},{112,96},{1... | collective-permute-start | bytes 1179656 | tf_op jit(solution)/shard_map/ppermute | solution.py:26
  70.0 9.7 %collective-permute-start.5 = (f32[128,768]{1,0:T(8,128)S(1)}, f32[128,768]{1,0:T(8,128)S(1)}, u32[]{:S(2)}, u32[]{:S(2)}) collective-permute-start(f32[128,768]{1,0:T(8,128)S(1)} %collective-permute-done.3), channel_id=1, source_target_pairs={{0,16},{16,32},{32,48},{48,64},{64,80},{80,96},{96,112},{112,0},{1... | collective-permute-start | bytes 1179656 | tf_op jit(solution)/shard_map/ppermute | solution.py:26
  74.2 8.4 %collective-permute-start.8 = (f32[64,768]{1,0:T(8,128)S(1)}, f32[64,768]{1,0:T(8,128)S(1)}, u32[]{:S(2)}, u32[]{:S(2)}) collective-permute-start(f32[64,768]{1,0:T(8,128)S(1)} %slice.75), channel_id=1, source_target_pairs={{0,112},{16,0},{32,16},{48,32},{64,48},{80,64},{96,80},{112,96},{1... | collective-permute-start | bytes 589832 | tf_op jit(solution)/shard_map/ppermute | solution.py:26
  79.7 7.6 %collective-permute-start.7 = (f32[64,768]{1,0:T(8,128)S(1)}, f32[64,768]{1,0:T(8,128)S(1)}, u32[]{:S(2)}, u32[]{:S(2)}) collective-permute-start(f32[64,768]{1,0:T(8,128)S(1)} %slice.73), channel_id=1, source_target_pairs={{0,16},{16,32},{32,48},{48,64},{64,80},{80,96},{96,112},{112,0},{1... | collective-permute-start | bytes 589832 | tf_op jit(solution)/shard_map/ppermute | solution.py:26
  88.4 10.2 %collective-permute-start.9 = (f32[256,768]{1,0:T(8,128)S(1)}, f32[256,768]{1,0:T(8,128)S(1)}, u32[]{:S(2)}, u32[]{:S(2)}) collective-permute-start(f32[256,768]{1,0:T(8,128)S(1)} %fusion.2), channel_id=1, source_target_pairs={{0,128},{128,0},{1,129},{129,1},{2,130},{130,2},{3,131},{131,3},{4... | collective-permute-start | bytes 2359304 | tf_op jit(solution)/shard_map/ppermute | solution.py:21
  98.2 8.1 %copy-start.3 = (s32[3]{0:T(128)S(1)}, s32[3]{0:T(128)}, u32[]{:S(2)}) copy-start(s32[3]{0:T(128)} %param.11) | copy-start | bytes 40
  99.5 30.1 %copy-start.1 = (f32[3,256,256]{2,1,0:T(8,128)S(1)}, f32[3,256,256]{2,1,0:T(8,128)}, u32[]{:S(2)}) copy-start(f32[3,256,256]{2,1,0:T(8,128)} %param.10) | copy-start | bytes 2359300
  99.5 30.1 %all-to-all-start.1 = ((f32[8,32,768]{2,1,0:T(8,128)}), f32[8,32,768]{2,1,0:T(8,128)S(1)}, u32[]{:S(2)}, u32[]{:S(2)}) async-start(f32[8,32,768]{2,1,0:T(8,128)} %bitcast.35), calls=%async_computation.1 | async-start | bytes 1572864 | tf_op jit(solution)/shard_map/all_to_all | solution.py:91

commit v3 on v2

--- a/solution.py
+++ b/solution.py
@@ -39,11 +39,6 @@
     yield n // 2, half, passed_on(down[half:], axis, -1)
 
 
-def in_order(mine, other, axis, dim):
-    first = lax.axis_index(axis) == 0
-    return jnp.stack([jnp.where(first, mine, other), jnp.where(first, other, mine)], axis=dim)
-
-
 def body(front_panel, solved_prev, right_side, front_window, inv_diag, owner_map):
     nblk, block, own = front_panel.shape
     _, width = solved_prev.shape
@@ -66,17 +61,17 @@
     )
     column = column.reshape(nx * own, nblk * block)
 
-    sources = in_order(near, got, "y_lo", 0).reshape(ny, nz, nx * own, width).transpose(1, 0, 3, 2)
+    sources = jnp.stack([near, got]).reshape(ny, nz, nx * own, width).transpose(1, 0, 3, 2)
     sources = sources.reshape(nz, ny, nhi, ncore, part, nx * own)
     kept, given = (
-        lax.dynamic_index_in_dim(sources, which, 3, keepdims=False)
-        .transpose(0, 2, 1, 3, 4)
-        .reshape(nz, nhi * ny * part, nx * own)
+        lax.dynamic_index_in_dim(sources, which, 3, keepdims=False).reshape(
+            nz, ny * nhi * part, nx * own
+        )
         for which in (core, ncore - 1 - core)
     )
     sides = lax.dynamic_slice_in_dim(right_side, here * part, part, axis=1).T
 
-    local = jnp.zeros((nhi * ny * part, nblk * block), jnp.float32)
+    local = jnp.zeros((ny * nhi * part, nblk * block), jnp.float32)
     others = local
     for offset, first, rows in ring(column, "z"):
         place = (lax.axis_index("z") + offset) % nz
@@ -88,9 +83,9 @@
         others += dot(given_rows, rows, ((1,), (0,)), HIGH)
         local += dot(kept_rows, rows, ((1,), (0,)), HIGH)
     local = lax.optimization_barrier(local) + swapped(others, "core")
-    pieces = lax.all_to_all(
-        local.reshape(nhi * ny, part, nblk * block), ("y_hi", "y_lo"), 0, 0, tiled=True
-    )
+    local = local.reshape(ny, nhi, part, nblk * block)
+    local = local[0] + swapped(local[1], "y_lo")
+    pieces = lax.all_to_all(local, "y_hi", 0, 0, tiled=True)
     rest = sides - pieces.sum(axis=0)
 
     slots = jnp.arange(groups, dtype=owner_map.dtype)[:, None, None]

time: 150 us -> 152 us (1.013)
  the two profiles are of different devices: /device:TPU:1 before, /device:TPU:16 now
where the time goes in v3:
time: 152 us; the launch traced here: 151 us
  starting transfers between devices  66.6 us (44%)
  waiting for transfers between devices  45.3 us (30%)
  blocking collectives  14.4 us (9%)
  matrix products  13.9 us (9%)
  local copies, waits for them, and re-layouts  6.43 us (4%)
  other arithmetic  4.26 us (3%)
    ppermute x8, starting transfers between devices, passed_on(): return lax.ppermute(value, axis, [(i, (i + step) % n) for i in range(n)])  35 us
    ppermute x3, starting transfers between devices, swapped(): return lax.ppermute(value, axis, [(0, 1), (1, 0)])  20.5 us
    all_to_all x1, blocking collectives, body(): stored = lax.all_to_all(routed, ROW, 0, 0, tiled=True)  14.4 us
    dot_general x24, matrix products, dot(): lax.dot_general(a, b, (dims, ((), ())), precision=precision, preferred_el...  13.9 us
    ppermute x8, waiting for transfers between devices, passed_on(): return lax.ppermute(value, axis, [(i, (i + step) % n) for i in range(n)])  13.5 us
    all_to_all x1, waiting for transfers between devices, body(): lax.all_to_all(jnp.broadcast_to(panel[None], (nx, *panel.shape)), 'x', 0,...  11.3 us
    all_to_all x1, waiting for transfers between devices, body(): pieces = lax.all_to_all(local, 'y_hi', 0, 0, tiled=True)  10.4 us
    ppermute x3, waiting for transfers between devices, swapped(): return lax.ppermute(value, axis, [(0, 1), (1, 0)])  10.1 us
  transfers between devices with their start and end apart: 13, of which 9 were waited for; matrix products, arithmetic and copies ran while one was open for 9% of the time, Pallas kernels for 0%

profile of v3, /device:TPU:16, one launch (start us, length us, event | category | flops | bytes accessed | tf_op | source)
XLA Modules:
  0.0 151.5 jit_solution(8734274481457419156)
XLA Ops:
  0.0 1.8 %constant_dynamic-slice_fusion.3 = (f32[8,1,128,256]{3,2,1,0:T(8,128)S(1)}, f32[8,1,128,256]{3,2,1,0:T(8,128)S(1)}) fusion(f32[8,2,128,256]{3,2,1,0:T(8,128)} %bitcast.122, s32[]{:T(128)S(6)} %select_n.100, s32[]{:T(128)S(6)} %select_n.101), kind=kLoop, calls=%fused_computation.98 | loop fusion | bytes 4194312 | tf_op jit(solution)/shard_map/jit(dynamic_index_in_dim)/dynamic_slice | solution.py:56
  1.8 1.3 copy.21
  3.2 14.9 %collective-permute-start = (f32[8,128,256]{1,2,0:T(8,128)}, f32[8,128,256]{1,2,0:T(8,128)}, u32[]{:S(2)}, u32[]{:S(2)}) collective-permute-start(f32[8,128,256]{1,2,0:T(8,128)} %bitcast.124), channel_id=1, source_target_pairs={{0,8},{8,0},{1,9},{9,1},{2,10},{10,2},{3,11},{11,3},{4,12},{12,4},... | collective-permute-start | bytes 3145736 | tf_op jit(solution)/shard_map/ppermute | solution.py:21
  18.8 3.5 %all-to-all-start = ((f32[8,16,768]{2,1,0:T(8,128)}), f32[8,16,768]{2,1,0:T(8,128)S(1)}, u32[]{:S(2)}, u32[]{:S(2)}) async-start(f32[8,16,768]{2,1,0:T(8,128)} %broadcast_in_dim.52), calls=%async_computation | async-start | bytes 786432 | tf_op jit(solution)/shard_map/all_to_all | solution.py:59
  22.8 11.3 %all-to-all-done = f32[8,16,768]{2,1,0:T(8,128)S(1)} async-done(((f32[8,16,768]{2,1,0:T(8,128)}), f32[8,16,768]{2,1,0:T(8,128)S(1)}, u32[]{:S(2)}, u32[]{:S(2)}) %all-to-all-start) | async-done | bytes 393248 | tf_op jit(solution)/shard_map/all_to_all | solution.py:59
  34.1 1.9 %collective-permute-start.1 = (f32[128,768]{1,0:T(8,128)S(1)}, f32[128,768]{1,0:T(8,128)S(1)}, u32[]{:S(2)}, u32[]{:S(2)}) collective-permute-start(f32[128,768]{1,0:T(8,128)S(1)} %bitcast.118), channel_id=1, source_target_pairs={{0,16},{16,32},{32,48},{48,64},{64,80},{80,96},{96,112},{112,0},{1... | collective-permute-start | bytes 1179656 | tf_op jit(solution)/shard_map/ppermute | solution.py:26
  36.0 10.6 %collective-permute-start.2 = (f32[128,768]{1,0:T(8,128)S(1)}, f32[128,768]{1,0:T(8,128)S(1)}, u32[]{:S(2)}, u32[]{:S(2)}) collective-permute-start(f32[128,768]{1,0:T(8,128)S(1)} %bitcast.119), channel_id=1, source_target_pairs={{0,112},{16,0},{32,16},{48,32},{64,48},{80,64},{96,80},{112,96},{1... | collective-permute-start | bytes 1179656 | tf_op jit(solution)/shard_map/ppermute | solution.py:26
  46.6 1.4 pad_maximum_fusion
  49.3 4.2 %collective-permute-done.2 = f32[128,768]{1,0:T(8,128)S(1)} collective-permute-done((f32[128,768]{1,0:T(8,128)S(1)}, f32[128,768]{1,0:T(8,128)S(1)}, u32[]{:S(2)}, u32[]{:S(2)}) %collective-permute-start.2) | collective-permute-done | bytes 393248 | tf_op jit(solution)/shard_map/ppermute | solution.py:26
  53.5 5.6 %collective-permute-start.4 = (f32[128,768]{1,0:T(8,128)S(1)}, f32[128,768]{1,0:T(8,128)S(1)}, u32[]{:S(2)}, u32[]{:S(2)}) collective-permute-start(f32[128,768]{1,0:T(8,128)S(1)} %collective-permute-done.2), channel_id=1, source_target_pairs={{0,112},{16,0},{32,16},{48,32},{64,48},{80,64},{96,80},{112,96},{1... | collective-permute-start | bytes 1179656 | tf_op jit(solution)/shard_map/ppermute | solution.py:26
  59.1 1.9 %collective-permute-start.3 = (f32[128,768]{1,0:T(8,128)S(1)}, f32[128,768]{1,0:T(8,128)S(1)}, u32[]{:S(2)}, u32[]{:S(2)}) collective-permute-start(f32[128,768]{1,0:T(8,128)S(1)} %collective-permute-done.1), channel_id=1, source_target_pairs={{0,16},{16,32},{32,48},{48,64},{64,80},{80,96},{96,112},{112,0},{1... | collective-permute-start | bytes 1179656 | tf_op jit(solution)/shard_map/ppermute | solution.py:26
  63.0 2.1 %collective-permute-done.4 = f32[128,768]{1,0:T(8,128)S(1)} collective-permute-done((f32[128,768]{1,0:T(8,128)S(1)}, f32[128,768]{1,0:T(8,128)S(1)}, u32[]{:S(2)}, u32[]{:S(2)}) %collective-permute-start.4) | collective-permute-done | bytes 393248 | tf_op jit(solution)/shard_map/ppermute | solution.py:26
  65.1 5.6 %collective-permute-start.6 = (f32[128,768]{1,0:T(8,128)S(1)}, f32[128,768]{1,0:T(8,128)S(1)}, u32[]{:S(2)}, u32[]{:S(2)}) collective-permute-start(f32[128,768]{1,0:T(8,128)S(1)} %collective-permute-done.4), channel_id=1, source_target_pairs={{0,112},{16,0},{32,16},{48,32},{64,48},{80,64},{96,80},{112,96},{1... | collective-permute-start | bytes 1179656 | tf_op jit(solution)/shard_map/ppermute | solution.py:26
  71.2 1.9 %collective-permute-start.5 = (f32[128,768]{1,0:T(8,128)S(1)}, f32[128,768]{1,0:T(8,128)S(1)}, u32[]{:S(2)}, u32[]{:S(2)}) collective-permute-start(f32[128,768]{1,0:T(8,128)S(1)} %collective-permute-done.3), channel_id=1, source_target_pairs={{0,16},{16,32},{32,48},{48,64},{64,80},{80,96},{96,112},{112,0},{1... | collective-permute-start | bytes 1179656 | tf_op jit(solution)/shard_map/ppermute | solution.py:26
  74.7 1.3 collective-permute-done.6
  76.0 5.6 %collective-permute-start.8 = (f32[64,768]{1,0:T(8,128)S(1)}, f32[64,768]{1,0:T(8,128)S(1)}, u32[]{:S(2)}, u32[]{:S(2)}) collective-permute-start(f32[64,768]{1,0:T(8,128)S(1)} %slice.85), channel_id=1, source_target_pairs={{0,112},{16,0},{32,16},{48,32},{64,48},{80,64},{96,80},{112,96},{1... | collective-permute-start | bytes 589832 | tf_op jit(solution)/shard_map/ppermute | solution.py:26
  82.1 1.9 %collective-permute-start.7 = (f32[64,768]{1,0:T(8,128)S(1)}, f32[64,768]{1,0:T(8,128)S(1)}, u32[]{:S(2)}, u32[]{:S(2)}) collective-permute-start(f32[64,768]{1,0:T(8,128)S(1)} %slice.83), channel_id=1, source_target_pairs={{0,16},{16,32},{32,48},{48,64},{64,80},{80,96},{96,112},{112,0},{1... | collective-permute-start | bytes 589832 | tf_op jit(solution)/shard_map/ppermute | solution.py:26
  85.6 5.3 %collective-permute-done.7 = f32[64,768]{1,0:T(8,128)S(1)} collective-permute-done((f32[64,768]{1,0:T(8,128)S(1)}, f32[64,768]{1,0:T(8,128)S(1)}, u32[]{:S(2)}, u32[]{:S(2)}) %collective-permute-start.7) | collective-permute-done | bytes 196640 | tf_op jit(solution)/shard_map/ppermute | solution.py:26
  92.0 1.9 %collective-permute-start.9 = (f32[256,768]{1,0:T(8,128)S(1)}, f32[256,768]{1,0:T(8,128)S(1)}, u32[]{:S(2)}, u32[]{:S(2)}) collective-permute-start(f32[256,768]{1,0:T(8,128)S(1)} %fusion.2), channel_id=1, source_target_pairs={{0,128},{128,0},{1,129},{129,1},{2,130},{130,2},{3,131},{131,3},{4... | collective-permute-start | bytes 2359304 | tf_op jit(solution)/shard_map/ppermute | solution.py:21
  96.3 3.8 %collective-permute-start.10 = (f32[4,32,768]{2,1,0:T(8,128)S(1)}, f32[4,32,768]{2,1,0:T(8,128)S(1)}, u32[]{:S(2)}, u32[]{:S(2)}) collective-permute-start(f32[4,32,768]{2,1,0:T(8,128)S(1)} %bitcast.126), channel_id=1, source_target_pairs={{0,8},{8,0},{1,9},{9,1},{2,10},{10,2},{3,11},{11,3},{4,12},{12,4},... | collective-permute-start | bytes 1179656 | tf_op jit(solution)/shard_map/ppermute | solution.py:21
  100.1 9.4 %collective-permute-done.10 = f32[4,32,768]{2,1,0:T(8,128)S(1)} collective-permute-done((f32[4,32,768]{2,1,0:T(8,128)S(1)}, f32[4,32,768]{2,1,0:T(8,128)S(1)}, u32[]{:S(2)}, u32[]{:S(2)}) %collective-permute-start.10) | collective-permute-done | bytes 393248 | tf_op jit(solution)/shard_map/ppermute | solution.py:21
  110.3 7.6 %all-to-all-start.1 = ((f32[4,32,768]{2,1,0:T(8,128)}), f32[4,32,768]{2,1,0:T(8,128)S(1)}, u32[]{:S(2)}, u32[]{:S(2)}) async-start(f32[4,32,768]{2,1,0:T(8,128)} %add.205), calls=%async_computation.1 | async-start | bytes 786432 | tf_op jit(solution)/shard_map/all_to_all | solution.py:88
  120.7 10.4 %all-to-all-done.1 = f32[4,32,768]{2,1,0:T(8,128)S(1)} async-done(((f32[4,32,768]{2,1,0:T(8,128)}), f32[4,32,768]{2,1,0:T(8,128)S(1)}, u32[]{:S(2)}, u32[]{:S(2)}) %all-to-all-start.1) | async-done | bytes 393248 | tf_op jit(solution)/shard_map/all_to_all | solution.py:88
  136.3 14.4 %all_to_all.15 = f32[8,32,256]{2,1,0:T(8,128)S(1)} all-to-all(f32[8,32,256]{2,1,0:T(8,128)S(1)} %select_select_fusion), channel_id=1, replica_groups=mesh['y_hi'=4,'core'=2,'z'=8,'y_lo'=2,'x'=8] {'y_hi','core'}, dimensions={0} | all-to-all | bytes 524288 | tf_op jit(solution)/shard_map/all_to_all | solution.py:102
  (57 shorter events, 21.2 us)
Async XLA Ops:
  0.0 117.9 %copy-start = (f32[768,256]{1,0:T(8,128)S(1)}, f32[768,256]{1,0:T(8,128)}, u32[]{:S(2)}) copy-start(f32[768,256]{1,0:T(8,128)} %param.8) | copy-start | bytes 2359300
  0.0 18.0 %copy-start.2 = (f32[3,256,16]{1,2,0:T(8,128)S(1)}, f32[3,256,16]{1,2,0:T(8,128)}, u32[]{:S(2)}) copy-start(f32[3,256,16]{1,2,0:T(8,128)} %param.6) | copy-start | bytes 147460
  3.2 43.4 %collective-permute-start = (f32[8,128,256]{1,2,0:T(8,128)}, f32[8,128,256]{1,2,0:T(8,128)}, u32[]{:S(2)}, u32[]{:S(2)}) collective-permute-start(f32[8,128,256]{1,2,0:T(8,128)} %bitcast.124), channel_id=1, source_target_pairs={{0,8},{8,0},{1,9},{9,1},{2,10},{10,2},{3,11},{11,3},{4,12},{12,4},... | collective-permute-start | bytes 3145736 | tf_op jit(solution)/shard_map/ppermute | solution.py:21
  18.8 15.3 %all-to-all-start = ((f32[8,16,768]{2,1,0:T(8,128)}), f32[8,16,768]{2,1,0:T(8,128)S(1)}, u32[]{:S(2)}, u32[]{:S(2)}) async-start(f32[8,16,768]{2,1,0:T(8,128)} %broadcast_in_dim.52), calls=%async_computation | async-start | bytes 786432 | tf_op jit(solution)/shard_map/all_to_all | solution.py:59
  34.1 25.0 %collective-permute-start.1 = (f32[128,768]{1,0:T(8,128)S(1)}, f32[128,768]{1,0:T(8,128)S(1)}, u32[]{:S(2)}, u32[]{:S(2)}) collective-permute-start(f32[128,768]{1,0:T(8,128)S(1)} %bitcast.118), channel_id=1, source_target_pairs={{0,16},{16,32},{32,48},{48,64},{64,80},{80,96},{96,112},{112,0},{1... | collective-permute-start | bytes 1179656 | tf_op jit(solution)/shard_map/ppermute | solution.py:26
  36.0 17.5 %collective-permute-start.2 = (f32[128,768]{1,0:T(8,128)S(1)}, f32[128,768]{1,0:T(8,128)S(1)}, u32[]{:S(2)}, u32[]{:S(2)}) collective-permute-start(f32[128,768]{1,0:T(8,128)S(1)} %bitcast.119), channel_id=1, source_target_pairs={{0,112},{16,0},{32,16},{48,32},{64,48},{80,64},{96,80},{112,96},{1... | collective-permute-start | bytes 1179656 | tf_op jit(solution)/shard_map/ppermute | solution.py:26
  53.5 11.6 %collective-permute-start.4 = (f32[128,768]{1,0:T(8,128)S(1)}, f32[128,768]{1,0:T(8,128)S(1)}, u32[]{:S(2)}, u32[]{:S(2)}) collective-permute-start(f32[128,768]{1,0:T(8,128)S(1)} %collective-permute-done.2), channel_id=1, source_target_pairs={{0,112},{16,0},{32,16},{48,32},{64,48},{80,64},{96,80},{112,96},{1... | collective-permute-start | bytes 1179656 | tf_op jit(solution)/shard_map/ppermute | solution.py:26
  59.1 12.1 %collective-permute-start.3 = (f32[128,768]{1,0:T(8,128)S(1)}, f32[128,768]{1,0:T(8,128)S(1)}, u32[]{:S(2)}, u32[]{:S(2)}) collective-permute-start(f32[128,768]{1,0:T(8,128)S(1)} %collective-permute-done.1), channel_id=1, source_target_pairs={{0,16},{16,32},{32,48},{48,64},{64,80},{80,96},{96,112},{112,0},{1... | collective-permute-start | bytes 1179656 | tf_op jit(solution)/shard_map/ppermute | solution.py:26
  65.1 10.9 %collective-permute-start.6 = (f32[128,768]{1,0:T(8,128)S(1)}, f32[128,768]{1,0:T(8,128)S(1)}, u32[]{:S(2)}, u32[]{:S(2)}) collective-permute-start(f32[128,768]{1,0:T(8,128)S(1)} %collective-permute-done.4), channel_id=1, source_target_pairs={{0,112},{16,0},{32,16},{48,32},{64,48},{80,64},{96,80},{112,96},{1... | collective-permute-start | bytes 1179656 | tf_op jit(solution)/shard_map/ppermute | solution.py:26
  71.2 10.9 %collective-permute-start.5 = (f32[128,768]{1,0:T(8,128)S(1)}, f32[128,768]{1,0:T(8,128)S(1)}, u32[]{:S(2)}, u32[]{:S(2)}) collective-permute-start(f32[128,768]{1,0:T(8,128)S(1)} %collective-permute-done.3), channel_id=1, source_target_pairs={{0,16},{16,32},{32,48},{48,64},{64,80},{80,96},{96,112},{112,0},{1... | collective-permute-start | bytes 1179656 | tf_op jit(solution)/shard_map/ppermute | solution.py:26
  76.0 9.0 %collective-permute-start.8 = (f32[64,768]{1,0:T(8,128)S(1)}, f32[64,768]{1,0:T(8,128)S(1)}, u32[]{:S(2)}, u32[]{:S(2)}) collective-permute-start(f32[64,768]{1,0:T(8,128)S(1)} %slice.85), channel_id=1, source_target_pairs={{0,112},{16,0},{32,16},{48,32},{64,48},{80,64},{96,80},{112,96},{1... | collective-permute-start | bytes 589832 | tf_op jit(solution)/shard_map/ppermute | solution.py:26
  82.1 8.8 %collective-permute-start.7 = (f32[64,768]{1,0:T(8,128)S(1)}, f32[64,768]{1,0:T(8,128)S(1)}, u32[]{:S(2)}, u32[]{:S(2)}) collective-permute-start(f32[64,768]{1,0:T(8,128)S(1)} %slice.83), channel_id=1, source_target_pairs={{0,16},{16,32},{32,48},{48,64},{64,80},{80,96},{96,112},{112,0},{1... | collective-permute-start | bytes 589832 | tf_op jit(solution)/shard_map/ppermute | solution.py:26
  92.0 4.2 %collective-permute-start.9 = (f32[256,768]{1,0:T(8,128)S(1)}, f32[256,768]{1,0:T(8,128)S(1)}, u32[]{:S(2)}, u32[]{:S(2)}) collective-permute-start(f32[256,768]{1,0:T(8,128)S(1)} %fusion.2), channel_id=1, source_target_pairs={{0,128},{128,0},{1,129},{129,1},{2,130},{130,2},{3,131},{131,3},{4... | collective-permute-start | bytes 2359304 | tf_op jit(solution)/shard_map/ppermute | solution.py:21
  96.2 21.9 %copy-start.3 = (s32[3]{0:T(128)S(1)}, s32[3]{0:T(128)}, u32[]{:S(2)}) copy-start(s32[3]{0:T(128)} %param.11) | copy-start | bytes 40
  96.3 34.9 %copy-start.1 = (f32[3,256,256]{2,1,0:T(8,128)S(1)}, f32[3,256,256]{2,1,0:T(8,128)}, u32[]{:S(2)}) copy-start(f32[3,256,256]{2,1,0:T(8,128)} %param.10) | copy-start | bytes 2359300
  96.3 13.2 %collective-permute-start.10 = (f32[4,32,768]{2,1,0:T(8,128)S(1)}, f32[4,32,768]{2,1,0:T(8,128)S(1)}, u32[]{:S(2)}, u32[]{:S(2)}) collective-permute-start(f32[4,32,768]{2,1,0:T(8,128)S(1)} %bitcast.126), channel_id=1, source_target_pairs={{0,8},{8,0},{1,9},{9,1},{2,10},{10,2},{3,11},{11,3},{4,12},{12,4},... | collective-permute-start | bytes 1179656 | tf_op jit(solution)/shard_map/ppermute | solution.py:21
  110.3 20.8 %all-to-all-start.1 = ((f32[4,32,768]{2,1,0:T(8,128)}), f32[4,32,768]{2,1,0:T(8,128)S(1)}, u32[]{:S(2)}, u32[]{:S(2)}) async-start(f32[4,32,768]{2,1,0:T(8,128)} %add.205), calls=%async_computation.1 | async-start | bytes 786432 | tf_op jit(solution)/shard_map/all_to_all | solution.py:88

commit v4 on v2

--- a/solution.py
+++ b/solution.py
@@ -42,6 +42,23 @@
 def in_order(mine, other, axis, dim):
     first = lax.axis_index(axis) == 0
     return jnp.stack([jnp.where(first, mine, other), jnp.where(first, other, mine)], axis=dim)
+
+
+def solve_operator(front_window, inv_diag):
+    nblk, block, _ = inv_diag.shape
+    rows = inv_diag[0]
+    for k in range(1, nblk):
+        window = front_window[k * block : (k + 1) * block, : k * block]
+        before = dot(window, rows, ((1,), (0,)), HIGHEST)
+        below = -dot(inv_diag[k], before, ((1,), (0,)), HIGHEST)
+        rows = jnp.concatenate(
+            [
+                jnp.pad(rows, ((0, 0), (0, block))),
+                jnp.concatenate([below, inv_diag[k]], axis=1),
+            ],
+            axis=0,
+        )
+    return rows
 
 
 def body(front_panel, solved_prev, right_side, front_window, inv_diag, owner_map):
@@ -93,16 +110,12 @@
     )
     rest = sides - pieces.sum(axis=0)
 
+    operator = lax.optimization_barrier(solve_operator(front_window, inv_diag))
+    solved = dot(rest, operator, ((1,), (1,)), HIGHEST)
     slots = jnp.arange(groups, dtype=owner_map.dtype)[:, None, None]
     routed = jnp.zeros((groups, part, block), jnp.float32)
-    solutions = []
     for k in range(nblk):
-        rhs = rest[:, k * block : (k + 1) * block]
-        for j, earlier in enumerate(solutions):
-            window = front_window[k * block : (k + 1) * block, j * block : (j + 1) * block]
-            rhs = rhs - dot(earlier, window, ((1,), (1,)), HIGHEST)
-        solution_k = dot(rhs, inv_diag[k], ((1,), (1,)), HIGHEST)
-        solutions.append(solution_k)
+        solution_k = solved[:, k * block : (k + 1) * block]
         routed = jnp.where(slots == owner_map[k], solution_k[None], routed)
     stored = lax.all_to_all(routed, ROW, 0, 0, tiled=True)
     return stored.reshape(width, block).T

time: 150 us -> 147 us (0.980)
  waiting for transfers between devices: 41.6 us -> 28.1 us
  local copies, waits for them, and re-layouts: 6.5 us -> 15.1 us
  other arithmetic: 4.62 us -> 6.14 us
    all_to_all x1, waiting for transfers between devices: 10.4 us -> 0.64 us  [body(): lax.all_to_all(jnp.broadcast_to(panel[None], (nx, *panel.shape)), 'x', 0,...]
    unnamed x11 -> x20, local copies, waits for them, and re-layouts: 1.8 us -> 7.67 us
    all_to_all x1, waiting for transfers between devices: 20.7 us -> 17 us  [body(): lax.all_to_all(local.reshape(nhi * ny, part, nblk * block), ('y_hi', 'y_l...]
    slice x0 -> x2, local copies, waits for them, and re-layouts: none -> 1.98 us  [the longest x1 1.97 us: solve_operator(): below = -dot(inv_diag[k], before, ((1,), (0,)), HIGHEST)]
    dot_general x24 -> x23, matrix products: 13.8 us -> 14.9 us  [dot(): lax.dot_general(a, b, (dims, ((), ())), precision=precision, preferred_el...]
  transfers between devices with their start and end apart: 12 -> 12, of which waited for: 8 -> 8; matrix products, arithmetic and copies ran while one was open for 9% -> 18% of each run, Pallas kernels for 0% -> 0%
where the time goes in v4:
time: 147 us; the launch traced here: 146 us
  starting transfers between devices  68.4 us (47%)
  waiting for transfers between devices  28.1 us (19%)
  local copies, waits for them, and re-layouts  15.1 us (10%)
  matrix products  14.9 us (10%)
  blocking collectives  13.2 us (9%)
  other arithmetic  6.14 us (4%)
    ppermute x8, starting transfers between devices, passed_on(): return lax.ppermute(value, axis, [(i, (i + step) % n) for i in range(n)])  43.1 us
    all_to_all x1, waiting for transfers between devices, body(): lax.all_to_all(local.reshape(nhi * ny, part, nblk * block), ('y_hi', 'y_l...  17 us
    dot_general x23, matrix products, dot(): lax.dot_general(a, b, (dims, ((), ())), precision=precision, preferred_el...  14.9 us
    all_to_all x1, blocking collectives, body(): stored = lax.all_to_all(routed, ROW, 0, 0, tiled=True)  13.2 us
    ppermute x2, starting transfers between devices, swapped(): return lax.ppermute(value, axis, [(0, 1), (1, 0)])  12.4 us
    ppermute x8, waiting for transfers between devices, passed_on(): return lax.ppermute(value, axis, [(i, (i + step) % n) for i in range(n)])  10.2 us
    unnamed x20, local copies, waits for them, and re-layouts  7.67 us
    all_to_all x1, starting transfers between devices, body(): lax.all_to_all(jnp.broadcast_to(panel[None], (nx, *panel.shape)), 'x', 0,...  6.48 us
  transfers between devices with their start and end apart: 12, of which 8 were waited for; matrix products, arithmetic and copies ran while one was open for 18% of the time, Pallas kernels for 0%

profile of v4, /device:TPU:1, one launch (start us, length us, event | category | flops | bytes accessed | tf_op | source)
XLA Modules:
  0.0 146.5 jit_solution(16593837657424221684)
XLA Ops:
  0.0 1.8 %constant_dynamic-slice_fusion.1 = (f32[8,1,128,256]{3,2,1,0:T(8,128)S(1)}, f32[8,1,128,256]{3,2,1,0:T(8,128)S(1)}) fusion(f32[8,2,128,256]{3,2,1,0:T(8,128)} %bitcast.146, s32[]{:T(128)S(6)} %select_n.113, s32[]{:T(128)S(6)} %select_n.114), kind=kLoop, calls=%fused_computation.100 | loop fusion | bytes 4194312 | tf_op jit(solution)/shard_map/jit(dynamic_index_in_dim)/dynamic_slice | solution.py:78
  3.2 4.1 %collective-permute-start = (f32[8,128,256]{1,2,0:T(8,128)}, f32[8,128,256]{1,2,0:T(8,128)}, u32[]{:S(2)}, u32[]{:S(2)}) collective-permute-start(f32[8,128,256]{1,2,0:T(8,128)} %bitcast.152), channel_id=1, source_target_pairs={{0,8},{8,0},{1,9},{9,1},{2,10},{10,2},{3,11},{11,3},{4,12},{12,4},... | collective-permute-start | bytes 3145736 | tf_op jit(solution)/shard_map/ppermute | solution.py:21
  8.1 6.5 %all-to-all-start = ((f32[8,16,768]{2,1,0:T(8,128)}), f32[8,16,768]{2,1,0:T(8,128)S(1)}, u32[]{:S(2)}, u32[]{:S(2)}) async-start(f32[8,16,768]{2,1,0:T(8,128)} %broadcast_in_dim.52), calls=%async_computation | async-start | bytes 786432 | tf_op jit(solution)/shard_map/all_to_all | solution.py:81
  15.9 1.8 %copy.42 = f32[768,32]{0,1:T(8,128)} copy(f32[768,32]{1,0:T(8,128)} %constant_dynamic-slice_fusion.2) | data formatting | bytes 196608
  17.7 2.0 %fusion.79 = (f32[1,256,256]{2,1,0:T(8,128)S(1)}, f32[1,256,256]{2,1,0:T(8,128)}, f32[1,256,256]{2,1,0:T(8,128)}) fusion(f32[3,256,256]{2,1,0:T(8,128)} %param.10), kind=kLoop, calls=%fused_computation.108 | loop fusion | bytes 1572864 | tf_op jit(solution)/shard_map/slice | solution.py:53
  20.7 1.8 %copy.46 = f32[1,256,256]{1,2,0:T(8,128)} copy(f32[1,256,256]{2,1,0:T(8,128)} %get-tuple-element.12) | data formatting | bytes 524288
  25.3 7.7 %collective-permute-start.1 = (f32[128,768]{1,0:T(8,128)S(1)}, f32[128,768]{1,0:T(8,128)S(1)}, u32[]{:S(2)}, u32[]{:S(2)}) collective-permute-start(f32[128,768]{1,0:T(8,128)S(1)} %bitcast.142), channel_id=1, source_target_pairs={{0,16},{16,32},{32,48},{48,64},{64,80},{80,96},{96,112},{112,0},{1... | collective-permute-start | bytes 1179656 | tf_op jit(solution)/shard_map/ppermute | solution.py:26
  33.0 14.1 %collective-permute-start.2 = (f32[128,768]{1,0:T(8,128)S(1)}, f32[128,768]{1,0:T(8,128)S(1)}, u32[]{:S(2)}, u32[]{:S(2)}) collective-permute-start(f32[128,768]{1,0:T(8,128)S(1)} %bitcast.143), channel_id=1, source_target_pairs={{0,112},{16,0},{32,16},{48,32},{64,48},{80,64},{96,80},{112,96},{1... | collective-permute-start | bytes 1179656 | tf_op jit(solution)/shard_map/ppermute | solution.py:26
  47.1 1.4 fusion.10
  50.2 3.3 %collective-permute-done.2 = f32[128,768]{1,0:T(8,128)S(1)} collective-permute-done((f32[128,768]{1,0:T(8,128)S(1)}, f32[128,768]{1,0:T(8,128)S(1)}, u32[]{:S(2)}, u32[]{:S(2)}) %collective-permute-start.2) | collective-permute-done | bytes 393248 | tf_op jit(solution)/shard_map/ppermute | solution.py:26
  53.4 5.3 %collective-permute-start.4 = (f32[128,768]{1,0:T(8,128)S(1)}, f32[128,768]{1,0:T(8,128)S(1)}, u32[]{:S(2)}, u32[]{:S(2)}) collective-permute-start(f32[128,768]{1,0:T(8,128)S(1)} %collective-permute-done.2), channel_id=1, source_target_pairs={{0,112},{16,0},{32,16},{48,32},{64,48},{80,64},{96,80},{112,96},{1... | collective-permute-start | bytes 1179656 | tf_op jit(solution)/shard_map/ppermute | solution.py:26
  58.7 1.9 %collective-permute-start.3 = (f32[128,768]{1,0:T(8,128)S(1)}, f32[128,768]{1,0:T(8,128)S(1)}, u32[]{:S(2)}, u32[]{:S(2)}) collective-permute-start(f32[128,768]{1,0:T(8,128)S(1)} %collective-permute-done.1), channel_id=1, source_target_pairs={{0,16},{16,32},{32,48},{48,64},{64,80},{80,96},{96,112},{112,0},{1... | collective-permute-start | bytes 1179656 | tf_op jit(solution)/shard_map/ppermute | solution.py:26
  62.7 1.5 %collective-permute-done.4 = f32[128,768]{1,0:T(8,128)S(1)} collective-permute-done((f32[128,768]{1,0:T(8,128)S(1)}, f32[128,768]{1,0:T(8,128)S(1)}, u32[]{:S(2)}, u32[]{:S(2)}) %collective-permute-start.4) | collective-permute-done | bytes 393248 | tf_op jit(solution)/shard_map/ppermute | solution.py:26
  64.2 5.3 %collective-permute-start.6 = (f32[128,768]{1,0:T(8,128)S(1)}, f32[128,768]{1,0:T(8,128)S(1)}, u32[]{:S(2)}, u32[]{:S(2)}) collective-permute-start(f32[128,768]{1,0:T(8,128)S(1)} %collective-permute-done.4), channel_id=1, source_target_pairs={{0,112},{16,0},{32,16},{48,32},{64,48},{80,64},{96,80},{112,96},{1... | collective-permute-start | bytes 1179656 | tf_op jit(solution)/shard_map/ppermute | solution.py:26
  70.0 1.9 %collective-permute-start.5 = (f32[128,768]{1,0:T(8,128)S(1)}, f32[128,768]{1,0:T(8,128)S(1)}, u32[]{:S(2)}, u32[]{:S(2)}) collective-permute-start(f32[128,768]{1,0:T(8,128)S(1)} %collective-permute-done.3), channel_id=1, source_target_pairs={{0,16},{16,32},{32,48},{48,64},{64,80},{80,96},{96,112},{112,0},{1... | collective-permute-start | bytes 1179656 | tf_op jit(solution)/shard_map/ppermute | solution.py:26
  74.2 5.0 %collective-permute-start.8 = (f32[64,768]{1,0:T(8,128)S(1)}, f32[64,768]{1,0:T(8,128)S(1)}, u32[]{:S(2)}, u32[]{:S(2)}) collective-permute-start(f32[64,768]{1,0:T(8,128)S(1)} %slice.73), channel_id=1, source_target_pairs={{0,112},{16,0},{32,16},{48,32},{64,48},{80,64},{96,80},{112,96},{1... | collective-permute-start | bytes 589832 | tf_op jit(solution)/shard_map/ppermute | solution.py:26
  79.8 1.9 %collective-permute-start.7 = (f32[64,768]{1,0:T(8,128)S(1)}, f32[64,768]{1,0:T(8,128)S(1)}, u32[]{:S(2)}, u32[]{:S(2)}) collective-permute-start(f32[64,768]{1,0:T(8,128)S(1)} %slice.71), channel_id=1, source_target_pairs={{0,16},{16,32},{32,48},{48,64},{64,80},{80,96},{96,112},{112,0},{1... | collective-permute-start | bytes 589832 | tf_op jit(solution)/shard_map/ppermute | solution.py:26
  83.2 4.2 %collective-permute-done.7 = f32[64,768]{1,0:T(8,128)S(1)} collective-permute-done((f32[64,768]{1,0:T(8,128)S(1)}, f32[64,768]{1,0:T(8,128)S(1)}, u32[]{:S(2)}, u32[]{:S(2)}) %collective-permute-start.7) | collective-permute-done | bytes 196640 | tf_op jit(solution)/shard_map/ppermute | solution.py:26
  88.4 8.3 %collective-permute-start.9 = (f32[256,768]{1,0:T(8,128)S(1)}, f32[256,768]{1,0:T(8,128)S(1)}, u32[]{:S(2)}, u32[]{:S(2)}) collective-permute-start(f32[256,768]{1,0:T(8,128)S(1)} %fusion.2), channel_id=1, source_target_pairs={{0,128},{128,0},{1,129},{129,1},{2,130},{130,2},{3,131},{131,3},{4... | collective-permute-start | bytes 2359304 | tf_op jit(solution)/shard_map/ppermute | solution.py:21
  99.6 6.4 %all-to-all-start.1 = ((f32[8,32,768]{2,1,0:T(8,128)}), f32[8,32,768]{2,1,0:T(8,128)}, u32[]{:S(2)}, u32[]{:S(2)}) async-start(f32[8,32,768]{2,1,0:T(8,128)} %bitcast.35), calls=%async_computation.1 | async-start | bytes 1572864 | tf_op jit(solution)/shard_map/all_to_all | solution.py:108
  106.8 2.1 %fusion.12 = f32[512,256]{1,0:T(8,128)S(1)} fusion(f32[768,768]{1,0:T(8,128)} %param.9, f32[256,256]{0,1:T(8,128)S(1)} %bitcast.149, f32[256,256]{0,1:T(8,128)S(1)} %bitcast.151, f32[256,256]{0,1:T(8,128)S(1)} %fusion.9), kind=kOutput, calls=%fused_computation.31 | convolution fusion | flops 806354944 | bytes 1835008 | tf_op jit(solution)/shard_map/dot_general | solution.py:15
  112.7 17.0 %all-to-all-done.1 = f32[8,32,768]{2,1,0:T(8,128)} async-done(((f32[8,32,768]{2,1,0:T(8,128)}), f32[8,32,768]{2,1,0:T(8,128)}, u32[]{:S(2)}, u32[]{:S(2)}) %all-to-all-start.1) | async-done | bytes 786464 | tf_op jit(solution)/shard_map/all_to_all | solution.py:108
  130.9 1.4 fusion.61
  132.5 13.2 %all_to_all.15 = f32[8,32,256]{2,1,0:T(8,128)S(1)} all-to-all(f32[8,32,256]{2,1,0:T(8,128)S(1)} %select_select_fusion), channel_id=1, replica_groups=mesh['y_hi'=4,'core'=2,'z'=8,'y_lo'=2,'x'=8] {'y_hi','core'}, dimensions={0} | all-to-all | bytes 524288 | tf_op jit(solution)/shard_map/all_to_all | solution.py:120
  (67 shorter events, 26.2 us)
Async XLA Ops:
  0.0 15.0 %copy-start = (f32[768,256]{1,0:T(8,128)S(1)}, f32[768,256]{1,0:T(8,128)}, u32[]{:S(2)}) copy-start(f32[768,256]{1,0:T(8,128)} %param.8) | copy-start | bytes 2359300
  0.0 7.3 %copy-start.5 = (f32[3,256,16]{1,2,0:T(8,128)S(1)}, f32[3,256,16]{1,2,0:T(8,128)}, u32[]{:S(2)}) copy-start(f32[3,256,16]{1,2,0:T(8,128)} %param.6) | copy-start | bytes 147460
  3.2 43.9 %collective-permute-start = (f32[8,128,256]{1,2,0:T(8,128)}, f32[8,128,256]{1,2,0:T(8,128)}, u32[]{:S(2)}, u32[]{:S(2)}) collective-permute-start(f32[8,128,256]{1,2,0:T(8,128)} %bitcast.152), channel_id=1, source_target_pairs={{0,8},{8,0},{1,9},{9,1},{2,10},{10,2},{3,11},{11,3},{4,12},{12,4},... | collective-permute-start | bytes 3145736 | tf_op jit(solution)/shard_map/ppermute | solution.py:21
  8.1 17.2 %all-to-all-start = ((f32[8,16,768]{2,1,0:T(8,128)}), f32[8,16,768]{2,1,0:T(8,128)S(1)}, u32[]{:S(2)}, u32[]{:S(2)}) async-start(f32[8,16,768]{2,1,0:T(8,128)} %broadcast_in_dim.52), calls=%async_computation | async-start | bytes 786432 | tf_op jit(solution)/shard_map/all_to_all | solution.py:81
  14.9 8.4 %copy-start.1 = (f32[3,256,256]{2,1,0:T(8,128)S(1)}, f32[3,256,256]{2,1,0:T(8,128)}, u32[]{:S(2)}) copy-start(f32[3,256,256]{2,1,0:T(8,128)} %param.10) | copy-start | bytes 2359300
  25.3 33.4 %collective-permute-start.1 = (f32[128,768]{1,0:T(8,128)S(1)}, f32[128,768]{1,0:T(8,128)S(1)}, u32[]{:S(2)}, u32[]{:S(2)}) collective-permute-start(f32[128,768]{1,0:T(8,128)S(1)} %bitcast.142), channel_id=1, source_target_pairs={{0,16},{16,32},{32,48},{48,64},{64,80},{80,96},{96,112},{112,0},{1... | collective-permute-start | bytes 1179656 | tf_op jit(solution)/shard_map/ppermute | solution.py:26
  33.0 20.4 %collective-permute-start.2 = (f32[128,768]{1,0:T(8,128)S(1)}, f32[128,768]{1,0:T(8,128)S(1)}, u32[]{:S(2)}, u32[]{:S(2)}) collective-permute-start(f32[128,768]{1,0:T(8,128)S(1)} %bitcast.143), channel_id=1, source_target_pairs={{0,112},{16,0},{32,16},{48,32},{64,48},{80,64},{96,80},{112,96},{1... | collective-permute-start | bytes 1179656 | tf_op jit(solution)/shard_map/ppermute | solution.py:26
  53.4 10.8 %collective-permute-start.4 = (f32[128,768]{1,0:T(8,128)S(1)}, f32[128,768]{1,0:T(8,128)S(1)}, u32[]{:S(2)}, u32[]{:S(2)}) collective-permute-start(f32[128,768]{1,0:T(8,128)S(1)} %collective-permute-done.2), channel_id=1, source_target_pairs={{0,112},{16,0},{32,16},{48,32},{64,48},{80,64},{96,80},{112,96},{1... | collective-permute-start | bytes 1179656 | tf_op jit(solution)/shard_map/ppermute | solution.py:26
  58.7 11.3 %collective-permute-start.3 = (f32[128,768]{1,0:T(8,128)S(1)}, f32[128,768]{1,0:T(8,128)S(1)}, u32[]{:S(2)}, u32[]{:S(2)}) collective-permute-start(f32[128,768]{1,0:T(8,128)S(1)} %collective-permute-done.1), channel_id=1, source_target_pairs={{0,16},{16,32},{32,48},{48,64},{64,80},{80,96},{96,112},{112,0},{1... | collective-permute-start | bytes 1179656 | tf_op jit(solution)/shard_map/ppermute | solution.py:26
  64.2 10.0 %collective-permute-start.6 = (f32[128,768]{1,0:T(8,128)S(1)}, f32[128,768]{1,0:T(8,128)S(1)}, u32[]{:S(2)}, u32[]{:S(2)}) collective-permute-start(f32[128,768]{1,0:T(8,128)S(1)} %collective-permute-done.4), channel_id=1, source_target_pairs={{0,112},{16,0},{32,16},{48,32},{64,48},{80,64},{96,80},{112,96},{1... | collective-permute-start | bytes 1179656 | tf_op jit(solution)/shard_map/ppermute | solution.py:26
  70.0 9.7 %collective-permute-start.5 = (f32[128,768]{1,0:T(8,128)S(1)}, f32[128,768]{1,0:T(8,128)S(1)}, u32[]{:S(2)}, u32[]{:S(2)}) collective-permute-start(f32[128,768]{1,0:T(8,128)S(1)} %collective-permute-done.3), channel_id=1, source_target_pairs={{0,16},{16,32},{32,48},{48,64},{64,80},{80,96},{96,112},{112,0},{1... | collective-permute-start | bytes 1179656 | tf_op jit(solution)/shard_map/ppermute | solution.py:26
  74.2 8.4 %collective-permute-start.8 = (f32[64,768]{1,0:T(8,128)S(1)}, f32[64,768]{1,0:T(8,128)S(1)}, u32[]{:S(2)}, u32[]{:S(2)}) collective-permute-start(f32[64,768]{1,0:T(8,128)S(1)} %slice.73), channel_id=1, source_target_pairs={{0,112},{16,0},{32,16},{48,32},{64,48},{80,64},{96,80},{112,96},{1... | collective-permute-start | bytes 589832 | tf_op jit(solution)/shard_map/ppermute | solution.py:26
  79.8 7.6 %collective-permute-start.7 = (f32[64,768]{1,0:T(8,128)S(1)}, f32[64,768]{1,0:T(8,128)S(1)}, u32[]{:S(2)}, u32[]{:S(2)}) collective-permute-start(f32[64,768]{1,0:T(8,128)S(1)} %slice.71), channel_id=1, source_target_pairs={{0,16},{16,32},{32,48},{48,64},{64,80},{80,96},{96,112},{112,0},{1... | collective-permute-start | bytes 589832 | tf_op jit(solution)/shard_map/ppermute | solution.py:26
  88.4 10.2 %collective-permute-start.9 = (f32[256,768]{1,0:T(8,128)S(1)}, f32[256,768]{1,0:T(8,128)S(1)}, u32[]{:S(2)}, u32[]{:S(2)}) collective-permute-start(f32[256,768]{1,0:T(8,128)S(1)} %fusion.2), channel_id=1, source_target_pairs={{0,128},{128,0},{1,129},{129,1},{2,130},{130,2},{3,131},{131,3},{4... | collective-permute-start | bytes 2359304 | tf_op jit(solution)/shard_map/ppermute | solution.py:21
  98.2 8.4 %copy-start.3 = (f32[1,256,256]{1,2,0:T(8,128)S(1)}, f32[1,256,256]{1,2,0:T(8,128)}, u32[]{:S(2)}) copy-start(f32[1,256,256]{1,2,0:T(8,128)} %copy.46) | copy-start | bytes 786436
  99.6 30.1 %all-to-all-start.1 = ((f32[8,32,768]{2,1,0:T(8,128)}), f32[8,32,768]{2,1,0:T(8,128)}, u32[]{:S(2)}, u32[]{:S(2)}) async-start(f32[8,32,768]{2,1,0:T(8,128)} %bitcast.35), calls=%async_computation.1 | async-start | bytes 1572864 | tf_op jit(solution)/shard_map/all_to_all | solution.py:108
  106.6 2.8 %copy-start.2 = (f32[1,256,256]{1,2,0:T(8,128)S(1)}, f32[1,256,256]{1,2,0:T(8,128)}, u32[]{:S(2)}) copy-start(f32[1,256,256]{1,2,0:T(8,128)} %copy.47) | copy-start | bytes 786436
  109.5 0.7 copy-start.6
  109.5 21.4 %copy-start.4 = (f32[768,32]{0,1:T(8,128)S(1)}, f32[768,32]{0,1:T(8,128)}, u32[]{:S(2)}) copy-start(f32[768,32]{0,1:T(8,128)} %copy.42) | copy-start | bytes 294916

commit v5 on v4

--- a/solution.py
+++ b/solution.py
@@ -32,7 +32,8 @@
     up = down = rows
     yield 0, 0, rows
     for step in range(1, n // 2):
-        up, down = passed_on(up, axis, 1), passed_on(down, axis, -1)
+        up = passed_on(up, axis, 1)
+        down = passed_on(down, axis, -1)
         yield -step, 0, up
         yield step, 0, down
     yield n // 2, 0, passed_on(up[:half], axis, 1)
@@ -83,7 +84,8 @@
     )
     column = column.reshape(nx * own, nblk * block)
 
-    sources = in_order(near, got, "y_lo", 0).reshape(ny, nz, nx * own, width).transpose(1, 0, 3, 2)
+    sources = in_order(near, got, "y_lo", 0)
+    sources = sources.reshape(ny, nz, nx * own, width).transpose(1, 0, 3, 2)
     sources = sources.reshape(nz, ny, nhi, ncore, part, nx * own)
     kept, given = (
         lax.dynamic_index_in_dim(sources, which, 3, keepdims=False)

time: 147 us -> 147 us (level)
  no operation moved by 1% of the time
where the time goes in v5:
time: 147 us; the launch traced here: 146 us
  starting transfers between devices  68.4 us (47%)
  waiting for transfers between devices  28.1 us (19%)
  local copies, waits for them, and re-layouts  15.1 us (10%)
  matrix products  14.9 us (10%)
  blocking collectives  13.2 us (9%)
  other arithmetic  6.14 us (4%)
    ppermute x8, starting transfers between devices, passed_on(): return lax.ppermute(value, axis, [(i, (i + step) % n) for i in range(n)])  43.1 us
    all_to_all x1, waiting for transfers between devices, body(): lax.all_to_all(local.reshape(nhi * ny, part, nblk * block), ('y_hi', 'y_l...  17 us
    dot_general x23, matrix products, dot(): lax.dot_general(a, b, (dims, ((), ())), precision=precision, preferred_el...  14.9 us
    all_to_all x1, blocking collectives, body(): stored = lax.all_to_all(routed, ROW, 0, 0, tiled=True)  13.2 us
    ppermute x2, starting transfers between devices, swapped(): return lax.ppermute(value, axis, [(0, 1), (1, 0)])  12.4 us
    ppermute x8, waiting for transfers between devices, passed_on(): return lax.ppermute(value, axis, [(i, (i + step) % n) for i in range(n)])  10.2 us
    unnamed x20, local copies, waits for them, and re-layouts  7.67 us
    all_to_all x1, starting transfers between devices, body(): lax.all_to_all(jnp.broadcast_to(panel[None], (nx, *panel.shape)), 'x', 0,...  6.48 us
  transfers between devices with their start and end apart: 12, of which 8 were waited for; matrix products, arithmetic and copies ran while one was open for 18% of the time, Pallas kernels for 0%

profile of v5, /device:TPU:1, one launch (start us, length us, event | category | flops | bytes accessed | tf_op | source)
XLA Modules:
  0.0 146.5 jit_solution(16593837657424221684)
XLA Ops:
  0.0 1.8 %constant_dynamic-slice_fusion.1 = (f32[8,1,128,256]{3,2,1,0:T(8,128)S(1)}, f32[8,1,128,256]{3,2,1,0:T(8,128)S(1)}) fusion(f32[8,2,128,256]{3,2,1,0:T(8,128)} %bitcast.146, s32[]{:T(128)S(6)} %select_n.113, s32[]{:T(128)S(6)} %select_n.114), kind=kLoop, calls=%fused_computation.100 | loop fusion | bytes 4194312 | tf_op jit(solution)/shard_map/jit(dynamic_index_in_dim)/dynamic_slice | solution.py:79
  3.2 4.1 %collective-permute-start = (f32[8,128,256]{1,2,0:T(8,128)}, f32[8,128,256]{1,2,0:T(8,128)}, u32[]{:S(2)}, u32[]{:S(2)}) collective-permute-start(f32[8,128,256]{1,2,0:T(8,128)} %bitcast.152), channel_id=1, source_target_pairs={{0,8},{8,0},{1,9},{9,1},{2,10},{10,2},{3,11},{11,3},{4,12},{12,4},... | collective-permute-start | bytes 3145736 | tf_op jit(solution)/shard_map/ppermute | solution.py:21
  8.1 6.5 %all-to-all-start = ((f32[8,16,768]{2,1,0:T(8,128)}), f32[8,16,768]{2,1,0:T(8,128)S(1)}, u32[]{:S(2)}, u32[]{:S(2)}) async-start(f32[8,16,768]{2,1,0:T(8,128)} %broadcast_in_dim.52), calls=%async_computation | async-start | bytes 786432 | tf_op jit(solution)/shard_map/all_to_all | solution.py:82
  15.9 1.8 %copy.42 = f32[768,32]{0,1:T(8,128)} copy(f32[768,32]{1,0:T(8,128)} %constant_dynamic-slice_fusion.2) | data formatting | bytes 196608
  17.7 2.0 %fusion.79 = (f32[1,256,256]{2,1,0:T(8,128)S(1)}, f32[1,256,256]{2,1,0:T(8,128)}, f32[1,256,256]{2,1,0:T(8,128)}) fusion(f32[3,256,256]{2,1,0:T(8,128)} %param.10), kind=kLoop, calls=%fused_computation.108 | loop fusion | bytes 1572864 | tf_op jit(solution)/shard_map/slice | solution.py:54
  20.7 1.8 %copy.46 = f32[1,256,256]{1,2,0:T(8,128)} copy(f32[1,256,256]{2,1,0:T(8,128)} %get-tuple-element.12) | data formatting | bytes 524288
  25.3 7.7 %collective-permute-start.1 = (f32[128,768]{1,0:T(8,128)S(1)}, f32[128,768]{1,0:T(8,128)S(1)}, u32[]{:S(2)}, u32[]{:S(2)}) collective-permute-start(f32[128,768]{1,0:T(8,128)S(1)} %bitcast.142), channel_id=1, source_target_pairs={{0,16},{16,32},{32,48},{48,64},{64,80},{80,96},{96,112},{112,0},{1... | collective-permute-start | bytes 1179656 | tf_op jit(solution)/shard_map/ppermute | solution.py:26
  33.0 14.1 %collective-permute-start.2 = (f32[128,768]{1,0:T(8,128)S(1)}, f32[128,768]{1,0:T(8,128)S(1)}, u32[]{:S(2)}, u32[]{:S(2)}) collective-permute-start(f32[128,768]{1,0:T(8,128)S(1)} %bitcast.143), channel_id=1, source_target_pairs={{0,112},{16,0},{32,16},{48,32},{64,48},{80,64},{96,80},{112,96},{1... | collective-permute-start | bytes 1179656 | tf_op jit(solution)/shard_map/ppermute | solution.py:26
  47.1 1.4 fusion.10
  50.2 3.3 %collective-permute-done.2 = f32[128,768]{1,0:T(8,128)S(1)} collective-permute-done((f32[128,768]{1,0:T(8,128)S(1)}, f32[128,768]{1,0:T(8,128)S(1)}, u32[]{:S(2)}, u32[]{:S(2)}) %collective-permute-start.2) | collective-permute-done | bytes 393248 | tf_op jit(solution)/shard_map/ppermute | solution.py:26
  53.4 5.3 %collective-permute-start.4 = (f32[128,768]{1,0:T(8,128)S(1)}, f32[128,768]{1,0:T(8,128)S(1)}, u32[]{:S(2)}, u32[]{:S(2)}) collective-permute-start(f32[128,768]{1,0:T(8,128)S(1)} %collective-permute-done.2), channel_id=1, source_target_pairs={{0,112},{16,0},{32,16},{48,32},{64,48},{80,64},{96,80},{112,96},{1... | collective-permute-start | bytes 1179656 | tf_op jit(solution)/shard_map/ppermute | solution.py:26
  58.7 1.9 %collective-permute-start.3 = (f32[128,768]{1,0:T(8,128)S(1)}, f32[128,768]{1,0:T(8,128)S(1)}, u32[]{:S(2)}, u32[]{:S(2)}) collective-permute-start(f32[128,768]{1,0:T(8,128)S(1)} %collective-permute-done.1), channel_id=1, source_target_pairs={{0,16},{16,32},{32,48},{48,64},{64,80},{80,96},{96,112},{112,0},{1... | collective-permute-start | bytes 1179656 | tf_op jit(solution)/shard_map/ppermute | solution.py:26
  62.7 1.5 %collective-permute-done.4 = f32[128,768]{1,0:T(8,128)S(1)} collective-permute-done((f32[128,768]{1,0:T(8,128)S(1)}, f32[128,768]{1,0:T(8,128)S(1)}, u32[]{:S(2)}, u32[]{:S(2)}) %collective-permute-start.4) | collective-permute-done | bytes 393248 | tf_op jit(solution)/shard_map/ppermute | solution.py:26
  64.2 5.3 %collective-permute-start.6 = (f32[128,768]{1,0:T(8,128)S(1)}, f32[128,768]{1,0:T(8,128)S(1)}, u32[]{:S(2)}, u32[]{:S(2)}) collective-permute-start(f32[128,768]{1,0:T(8,128)S(1)} %collective-permute-done.4), channel_id=1, source_target_pairs={{0,112},{16,0},{32,16},{48,32},{64,48},{80,64},{96,80},{112,96},{1... | collective-permute-start | bytes 1179656 | tf_op jit(solution)/shard_map/ppermute | solution.py:26
  70.0 1.9 %collective-permute-start.5 = (f32[128,768]{1,0:T(8,128)S(1)}, f32[128,768]{1,0:T(8,128)S(1)}, u32[]{:S(2)}, u32[]{:S(2)}) collective-permute-start(f32[128,768]{1,0:T(8,128)S(1)} %collective-permute-done.3), channel_id=1, source_target_pairs={{0,16},{16,32},{32,48},{48,64},{64,80},{80,96},{96,112},{112,0},{1... | collective-permute-start | bytes 1179656 | tf_op jit(solution)/shard_map/ppermute | solution.py:26
  74.2 5.0 %collective-permute-start.8 = (f32[64,768]{1,0:T(8,128)S(1)}, f32[64,768]{1,0:T(8,128)S(1)}, u32[]{:S(2)}, u32[]{:S(2)}) collective-permute-start(f32[64,768]{1,0:T(8,128)S(1)} %slice.73), channel_id=1, source_target_pairs={{0,112},{16,0},{32,16},{48,32},{64,48},{80,64},{96,80},{112,96},{1... | collective-permute-start | bytes 589832 | tf_op jit(solution)/shard_map/ppermute | solution.py:26
  79.8 1.9 %collective-permute-start.7 = (f32[64,768]{1,0:T(8,128)S(1)}, f32[64,768]{1,0:T(8,128)S(1)}, u32[]{:S(2)}, u32[]{:S(2)}) collective-permute-start(f32[64,768]{1,0:T(8,128)S(1)} %slice.71), channel_id=1, source_target_pairs={{0,16},{16,32},{32,48},{48,64},{64,80},{80,96},{96,112},{112,0},{1... | collective-permute-start | bytes 589832 | tf_op jit(solution)/shard_map/ppermute | solution.py:26
  83.2 4.2 %collective-permute-done.7 = f32[64,768]{1,0:T(8,128)S(1)} collective-permute-done((f32[64,768]{1,0:T(8,128)S(1)}, f32[64,768]{1,0:T(8,128)S(1)}, u32[]{:S(2)}, u32[]{:S(2)}) %collective-permute-start.7) | collective-permute-done | bytes 196640 | tf_op jit(solution)/shard_map/ppermute | solution.py:26
  88.4 8.3 %collective-permute-start.9 = (f32[256,768]{1,0:T(8,128)S(1)}, f32[256,768]{1,0:T(8,128)S(1)}, u32[]{:S(2)}, u32[]{:S(2)}) collective-permute-start(f32[256,768]{1,0:T(8,128)S(1)} %fusion.2), channel_id=1, source_target_pairs={{0,128},{128,0},{1,129},{129,1},{2,130},{130,2},{3,131},{131,3},{4... | collective-permute-start | bytes 2359304 | tf_op jit(solution)/shard_map/ppermute | solution.py:21
  99.6 6.4 %all-to-all-start.1 = ((f32[8,32,768]{2,1,0:T(8,128)}), f32[8,32,768]{2,1,0:T(8,128)}, u32[]{:S(2)}, u32[]{:S(2)}) async-start(f32[8,32,768]{2,1,0:T(8,128)} %bitcast.35), calls=%async_computation.1 | async-start | bytes 1572864 | tf_op jit(solution)/shard_map/all_to_all | solution.py:110
  106.8 2.1 %fusion.12 = f32[512,256]{1,0:T(8,128)S(1)} fusion(f32[768,768]{1,0:T(8,128)} %param.9, f32[256,256]{0,1:T(8,128)S(1)} %bitcast.149, f32[256,256]{0,1:T(8,128)S(1)} %bitcast.151, f32[256,256]{0,1:T(8,128)S(1)} %fusion.9), kind=kOutput, calls=%fused_computation.31 | convolution fusion | flops 806354944 | bytes 1835008 | tf_op jit(solution)/shard_map/dot_general | solution.py:15
  112.7 17.0 %all-to-all-done.1 = f32[8,32,768]{2,1,0:T(8,128)} async-done(((f32[8,32,768]{2,1,0:T(8,128)}), f32[8,32,768]{2,1,0:T(8,128)}, u32[]{:S(2)}, u32[]{:S(2)}) %all-to-all-start.1) | async-done | bytes 786464 | tf_op jit(solution)/shard_map/all_to_all | solution.py:110
  130.9 1.4 fusion.61
  132.5 13.2 %all_to_all.15 = f32[8,32,256]{2,1,0:T(8,128)S(1)} all-to-all(f32[8,32,256]{2,1,0:T(8,128)S(1)} %select_select_fusion), channel_id=1, replica_groups=mesh['y_hi'=4,'core'=2,'z'=8,'y_lo'=2,'x'=8] {'y_hi','core'}, dimensions={0} | all-to-all | bytes 524288 | tf_op jit(solution)/shard_map/all_to_all | solution.py:122
  (67 shorter events, 26.2 us)
Async XLA Ops:
  0.0 15.0 %copy-start = (f32[768,256]{1,0:T(8,128)S(1)}, f32[768,256]{1,0:T(8,128)}, u32[]{:S(2)}) copy-start(f32[768,256]{1,0:T(8,128)} %param.8) | copy-start | bytes 2359300
  0.0 7.3 %copy-start.5 = (f32[3,256,16]{1,2,0:T(8,128)S(1)}, f32[3,256,16]{1,2,0:T(8,128)}, u32[]{:S(2)}) copy-start(f32[3,256,16]{1,2,0:T(8,128)} %param.6) | copy-start | bytes 147460
  3.2 43.9 %collective-permute-start = (f32[8,128,256]{1,2,0:T(8,128)}, f32[8,128,256]{1,2,0:T(8,128)}, u32[]{:S(2)}, u32[]{:S(2)}) collective-permute-start(f32[8,128,256]{1,2,0:T(8,128)} %bitcast.152), channel_id=1, source_target_pairs={{0,8},{8,0},{1,9},{9,1},{2,10},{10,2},{3,11},{11,3},{4,12},{12,4},... | collective-permute-start | bytes 3145736 | tf_op jit(solution)/shard_map/ppermute | solution.py:21
  8.1 17.2 %all-to-all-start = ((f32[8,16,768]{2,1,0:T(8,128)}), f32[8,16,768]{2,1,0:T(8,128)S(1)}, u32[]{:S(2)}, u32[]{:S(2)}) async-start(f32[8,16,768]{2,1,0:T(8,128)} %broadcast_in_dim.52), calls=%async_computation | async-start | bytes 786432 | tf_op jit(solution)/shard_map/all_to_all | solution.py:82
  14.9 8.4 %copy-start.1 = (f32[3,256,256]{2,1,0:T(8,128)S(1)}, f32[3,256,256]{2,1,0:T(8,128)}, u32[]{:S(2)}) copy-start(f32[3,256,256]{2,1,0:T(8,128)} %param.10) | copy-start | bytes 2359300
  25.3 33.4 %collective-permute-start.1 = (f32[128,768]{1,0:T(8,128)S(1)}, f32[128,768]{1,0:T(8,128)S(1)}, u32[]{:S(2)}, u32[]{:S(2)}) collective-permute-start(f32[128,768]{1,0:T(8,128)S(1)} %bitcast.142), channel_id=1, source_target_pairs={{0,16},{16,32},{32,48},{48,64},{64,80},{80,96},{96,112},{112,0},{1... | collective-permute-start | bytes 1179656 | tf_op jit(solution)/shard_map/ppermute | solution.py:26
  33.0 20.4 %collective-permute-start.2 = (f32[128,768]{1,0:T(8,128)S(1)}, f32[128,768]{1,0:T(8,128)S(1)}, u32[]{:S(2)}, u32[]{:S(2)}) collective-permute-start(f32[128,768]{1,0:T(8,128)S(1)} %bitcast.143), channel_id=1, source_target_pairs={{0,112},{16,0},{32,16},{48,32},{64,48},{80,64},{96,80},{112,96},{1... | collective-permute-start | bytes 1179656 | tf_op jit(solution)/shard_map/ppermute | solution.py:26
  53.4 10.8 %collective-permute-start.4 = (f32[128,768]{1,0:T(8,128)S(1)}, f32[128,768]{1,0:T(8,128)S(1)}, u32[]{:S(2)}, u32[]{:S(2)}) collective-permute-start(f32[128,768]{1,0:T(8,128)S(1)} %collective-permute-done.2), channel_id=1, source_target_pairs={{0,112},{16,0},{32,16},{48,32},{64,48},{80,64},{96,80},{112,96},{1... | collective-permute-start | bytes 1179656 | tf_op jit(solution)/shard_map/ppermute | solution.py:26
  58.7 11.3 %collective-permute-start.3 = (f32[128,768]{1,0:T(8,128)S(1)}, f32[128,768]{1,0:T(8,128)S(1)}, u32[]{:S(2)}, u32[]{:S(2)}) collective-permute-start(f32[128,768]{1,0:T(8,128)S(1)} %collective-permute-done.1), channel_id=1, source_target_pairs={{0,16},{16,32},{32,48},{48,64},{64,80},{80,96},{96,112},{112,0},{1... | collective-permute-start | bytes 1179656 | tf_op jit(solution)/shard_map/ppermute | solution.py:26
  64.2 10.0 %collective-permute-start.6 = (f32[128,768]{1,0:T(8,128)S(1)}, f32[128,768]{1,0:T(8,128)S(1)}, u32[]{:S(2)}, u32[]{:S(2)}) collective-permute-start(f32[128,768]{1,0:T(8,128)S(1)} %collective-permute-done.4), channel_id=1, source_target_pairs={{0,112},{16,0},{32,16},{48,32},{64,48},{80,64},{96,80},{112,96},{1... | collective-permute-start | bytes 1179656 | tf_op jit(solution)/shard_map/ppermute | solution.py:26
  70.0 9.7 %collective-permute-start.5 = (f32[128,768]{1,0:T(8,128)S(1)}, f32[128,768]{1,0:T(8,128)S(1)}, u32[]{:S(2)}, u32[]{:S(2)}) collective-permute-start(f32[128,768]{1,0:T(8,128)S(1)} %collective-permute-done.3), channel_id=1, source_target_pairs={{0,16},{16,32},{32,48},{48,64},{64,80},{80,96},{96,112},{112,0},{1... | collective-permute-start | bytes 1179656 | tf_op jit(solution)/shard_map/ppermute | solution.py:26
  74.2 8.4 %collective-permute-start.8 = (f32[64,768]{1,0:T(8,128)S(1)}, f32[64,768]{1,0:T(8,128)S(1)}, u32[]{:S(2)}, u32[]{:S(2)}) collective-permute-start(f32[64,768]{1,0:T(8,128)S(1)} %slice.73), channel_id=1, source_target_pairs={{0,112},{16,0},{32,16},{48,32},{64,48},{80,64},{96,80},{112,96},{1... | collective-permute-start | bytes 589832 | tf_op jit(solution)/shard_map/ppermute | solution.py:26
  79.8 7.6 %collective-permute-start.7 = (f32[64,768]{1,0:T(8,128)S(1)}, f32[64,768]{1,0:T(8,128)S(1)}, u32[]{:S(2)}, u32[]{:S(2)}) collective-permute-start(f32[64,768]{1,0:T(8,128)S(1)} %slice.71), channel_id=1, source_target_pairs={{0,16},{16,32},{32,48},{48,64},{64,80},{80,96},{96,112},{112,0},{1... | collective-permute-start | bytes 589832 | tf_op jit(solution)/shard_map/ppermute | solution.py:26
  88.4 10.2 %collective-permute-start.9 = (f32[256,768]{1,0:T(8,128)S(1)}, f32[256,768]{1,0:T(8,128)S(1)}, u32[]{:S(2)}, u32[]{:S(2)}) collective-permute-start(f32[256,768]{1,0:T(8,128)S(1)} %fusion.2), channel_id=1, source_target_pairs={{0,128},{128,0},{1,129},{129,1},{2,130},{130,2},{3,131},{131,3},{4... | collective-permute-start | bytes 2359304 | tf_op jit(solution)/shard_map/ppermute | solution.py:21
  98.2 8.4 %copy-start.3 = (f32[1,256,256]{1,2,0:T(8,128)S(1)}, f32[1,256,256]{1,2,0:T(8,128)}, u32[]{:S(2)}) copy-start(f32[1,256,256]{1,2,0:T(8,128)} %copy.46) | copy-start | bytes 786436
  99.6 30.1 %all-to-all-start.1 = ((f32[8,32,768]{2,1,0:T(8,128)}), f32[8,32,768]{2,1,0:T(8,128)}, u32[]{:S(2)}, u32[]{:S(2)}) async-start(f32[8,32,768]{2,1,0:T(8,128)} %bitcast.35), calls=%async_computation.1 | async-start | bytes 1572864 | tf_op jit(solution)/shard_map/all_to_all | solution.py:110
  106.6 2.8 %copy-start.2 = (f32[1,256,256]{1,2,0:T(8,128)S(1)}, f32[1,256,256]{1,2,0:T(8,128)}, u32[]{:S(2)}) copy-start(f32[1,256,256]{1,2,0:T(8,128)} %copy.47) | copy-start | bytes 786436
  109.5 0.7 copy-start.6
  109.5 21.4 %copy-start.4 = (f32[768,32]{0,1:T(8,128)S(1)}, f32[768,32]{0,1:T(8,128)}, u32[]{:S(2)}) copy-start(f32[768,32]{0,1:T(8,128)} %copy.42) | copy-start | bytes 294916
